TPU v7x, 32 devices: a whole 2x2x4 slice. The times are simulated.
32 devices in a mesh: dp: 32 (over z, y, x, core).
Axes of the slice: x: 2, y: 2, z: 4, core: 2. Of those that a mesh axis runs over, the one named last changes fastest.
Arguments:
- byte_inputs: bfloat16 [64, 2048, 768], P('dp'), may hold values from -6 to 6
- lengths: int32 [64], P('dp'), may hold values from 512 to 2048, as said below
- key_mask: int32 [64, 2048], P('dp'), may hold values from 0 to 1, as said below
- latents_cot: bfloat16 [64, 256, 1280], P('dp'), may hold values from -6 to 6
- latent_array: bfloat16 [256, 1280], P('dp'), may hold values from -6 to 6
- lat_gain: bfloat16 [1280], P('dp'), may hold values from 0.099609375 to 1.8984375
- query_weight: bfloat16 [1280, 768], P('dp'), may hold values from -0.3125 to 0.3125
- in_gain: bfloat16 [768], P('dp'), may hold values from 0.099609375 to 1.8984375
- key_weight: bfloat16 [768, 768], P('dp'), may hold values from -0.21875 to 0.21875
- value_weight: bfloat16 [768, 768], P('dp'), may hold values from -0.21875 to 0.21875
- out_weight: bfloat16 [768, 1280], P('dp'), may hold values from -1.75 to 1.75
- mlp_gain: bfloat16 [1280], P('dp'), may hold values from 0.099609375 to 1.8984375
- mlp_in_weight: bfloat16 [1280, 1280], P('dp'), may hold values from -0.15625 to 0.15625
- mlp_out_weight: bfloat16 [1280, 1280], P('dp'), may hold values from -0.15625 to 0.15625
Outputs:
- latents: bfloat16 [64, 256, 1280], P('dp')
- inputs_grad: bfloat16 [64, 2048, 768], P('dp')
- latent_array_grad: float32 [256, 1280], P('dp')
- lat_gain_grad: float32 [1280], P('dp')
- query_weight_grad: float32 [1280, 768], P('dp')
- in_gain_grad: float32 [768], P('dp')
- key_weight_grad: float32 [768, 768], P('dp')
- value_weight_grad: float32 [768, 768], P('dp')
- out_weight_grad: float32 [768, 1280], P('dp')
- mlp_gain_grad: float32 [1280], P('dp')
- mlp_in_weight_grad: float32 [1280, 1280], P('dp')
- mlp_out_weight_grad: float32 [1280, 1280], P('dp')
Inputs may be any that keep to these rules, and one draw needn't show every extreme that they name: `lengths`: sequence 0 has 2048 used slots; every other has 512, 1024 or 2048. `key_mask`: slot 0 of every sequence is 1.
All inputs are finite; a program needn't handle non-finite values.
Results may differ from a plain program's by a relative error of at most 0.014.
The roundings to bfloat16 on the way count: a program that leaves them out, or rounds other values in their place, can miss the bound.
Values may be sent and summed in bfloat16 or wider, within the bound.
No kernel may reach another device: no remote copies, remote signals or barrier semaphores. Data moves between devices by JAX's collectives and lax.ppermute only.
A program may use at most 320 MiB of HBM per device.

v0:
```python
import math

import jax
import jax.numpy as jnp
from jax import lax
from jax.sharding import PartitionSpec as P

HEADS = 8


def layer_norm(value_rows, gain):
    centred = value_rows - jnp.mean(value_rows, axis=-1, keepdims=True)
    inverse = lax.rsqrt(jnp.mean(centred * centred, axis=-1, keepdims=True) + 1e-05)
    unit = centred * inverse
    return (unit * gain, unit, inverse)


def norm_back(upstream, unit, inverse, gain):
    scaled = upstream * gain
    lead = tuple(range(upstream.ndim - 1))
    gain_grad = jnp.sum(upstream * unit, axis=lead)
    inner = (
        scaled
        - jnp.mean(scaled, axis=-1, keepdims=True)
        - unit * jnp.mean(scaled * unit, axis=-1, keepdims=True)
    )
    return (inverse * inner, gain_grad)


def gelu_slope(value_rows):
    cdf = 0.5 * (1.0 + jax.scipy.special.erf(value_rows * (1.0 / math.sqrt(2.0))))
    return cdf + value_rows * jnp.exp(-0.5 * value_rows * value_rows) * (
        1.0 / math.sqrt(2.0 * math.pi)
    )


def local(
    byte_inputs,
    lengths,
    key_mask,
    latents_cot,
    latent_array,
    lat_gain,
    query_weight,
    in_gain,
    key_weight,
    value_weight,
    out_weight,
    mlp_gain,
    mlp_in_weight,
    mlp_out_weight,
):
    single_float = jnp.float32
    brain_float_half = jnp.bfloat16
    attn_params = (
        lax.all_gather(latent_array, "dp", axis=0, tiled=True),
        lax.all_gather(lat_gain, "dp", axis=0, tiled=True),
        lax.all_gather(query_weight, "dp", axis=0, tiled=True),
        lax.all_gather(in_gain, "dp", axis=0, tiled=True),
        lax.all_gather(key_weight, "dp", axis=0, tiled=True),
        lax.all_gather(value_weight, "dp", axis=0, tiled=True),
        lax.all_gather(out_weight, "dp", axis=0, tiled=True),
    )
    mlp_params = (
        lax.all_gather(mlp_gain, "dp", axis=0, tiled=True),
        lax.all_gather(mlp_in_weight, "dp", axis=0, tiled=True),
        lax.all_gather(mlp_out_weight, "dp", axis=0, tiled=True),
    )
    base, g_lat, w_query, g_in, key_projection, value_projection, w_out = attn_params
    g_mlp, w_in, w_back = mlp_params
    seqs, length, width_in = byte_inputs.shape
    latent_rows = base.shape[0]
    head_dim = width_in // HEADS
    factor = 1.0 / math.sqrt(head_dim)
    base32 = base.astype(single_float)
    lat_normed, lat_unit, lat_inv = layer_norm(base32, g_lat.astype(single_float))
    lat_b = lat_normed.astype(brain_float_half)
    query = jnp.dot(lat_b, w_query, preferred_element_type=single_float).astype(brain_float_half)
    in_normed, in_unit, in_inv = layer_norm(
        byte_inputs.astype(single_float), g_in.astype(single_float)
    )
    input_normed_bf = in_normed.astype(brain_float_half)
    key_rows = jnp.einsum(
        "wrc,ca->wra", input_normed_bf, key_projection, preferred_element_type=single_float
    ).astype(brain_float_half)
    value_rows = jnp.einsum(
        "wrc,ca->wra", input_normed_bf, value_projection, preferred_element_type=single_float
    ).astype(brain_float_half)
    positions = jnp.arange(length, dtype=jnp.int32)
    valid = (positions[None, :] < lengths[:, None]) & (key_mask == 1)
    query_heads = query.reshape(latent_rows, HEADS, head_dim)
    key_heads = key_rows.reshape(seqs, length, HEADS, head_dim)
    value_heads = value_rows.reshape(seqs, length, HEADS, head_dim)

    def scores_of():
        raw = (
            jnp.einsum(
                "ihe,sjhe->shij", query_heads, key_heads, preferred_element_type=single_float
            )
            * factor
        )
        return jnp.where(valid[:, None, None, :], raw, -1e30)

    scores = scores_of()
    top = jnp.max(scores, axis=-1, keepdims=True)
    lse = top + jnp.log(jnp.sum(jnp.exp(scores - top), axis=-1, keepdims=True))
    probs_b = jnp.exp(scores - lse).astype(brain_float_half)
    mixed = (
        jnp.einsum("shij,sjhe->sihe", probs_b, value_heads, preferred_element_type=single_float)
        .reshape(seqs, latent_rows, width_in)
        .astype(brain_float_half)
    )
    x_one = base32[None] + jnp.einsum(
        "sie,ef->sif", mixed, w_out, preferred_element_type=single_float
    )
    mlp_normed, mlp_unit, mlp_inv = layer_norm(x_one, g_mlp.astype(single_float))
    mlp_b = mlp_normed.astype(brain_float_half)
    pre = jnp.einsum("sid,dh->sih", mlp_b, w_in, preferred_element_type=single_float)
    act = jax.nn.gelu(pre, approximate=False).astype(brain_float_half)
    latents = (
        x_one + jnp.einsum("sih,hf->sif", act, w_back, preferred_element_type=single_float)
    ).astype(brain_float_half)
    attn_again = (
        lax.all_gather(latent_array, "dp", axis=0, tiled=True),
        lax.all_gather(lat_gain, "dp", axis=0, tiled=True),
        lax.all_gather(query_weight, "dp", axis=0, tiled=True),
        lax.all_gather(in_gain, "dp", axis=0, tiled=True),
        lax.all_gather(key_weight, "dp", axis=0, tiled=True),
        lax.all_gather(value_weight, "dp", axis=0, tiled=True),
        lax.all_gather(out_weight, "dp", axis=0, tiled=True),
    )
    mlp_again = (
        lax.all_gather(mlp_gain, "dp", axis=0, tiled=True),
        lax.all_gather(mlp_in_weight, "dp", axis=0, tiled=True),
        lax.all_gather(mlp_out_weight, "dp", axis=0, tiled=True),
    )
    base, g_lat, w_query, g_in, key_projection, value_projection, w_out = attn_again
    g_mlp, w_in, w_back = mlp_again
    cot32 = latents_cot.astype(single_float)
    grad_back = jnp.einsum("sih,sif->hf", act, latents_cot, preferred_element_type=single_float)
    d_act = jnp.einsum("sif,hf->sih", latents_cot, w_back, preferred_element_type=single_float)
    d_pre = (d_act * gelu_slope(pre)).astype(brain_float_half)
    grad_in = jnp.einsum("sid,sih->dh", mlp_b, d_pre, preferred_element_type=single_float)
    d_mlpnorm = jnp.einsum("sih,dh->sid", d_pre, w_in, preferred_element_type=single_float)
    d_x_part, grad_gmlp = norm_back(d_mlpnorm, mlp_unit, mlp_inv, g_mlp.astype(single_float))
    d_x_one = cot32 + d_x_part
    d_attn = d_x_one.astype(brain_float_half)
    grad_out = jnp.einsum("sie,sif->ef", mixed, d_attn, preferred_element_type=single_float)
    d_mixed = jnp.einsum("sif,ef->sie", d_attn, w_out, preferred_element_type=single_float).astype(
        brain_float_half
    )
    d_mixed_heads = d_mixed.reshape(seqs, latent_rows, HEADS, head_dim)
    values_gradient = (
        jnp.einsum("shij,sihe->sjhe", probs_b, d_mixed_heads, preferred_element_type=single_float)
        .reshape(seqs, length, width_in)
        .astype(brain_float_half)
    )
    probs_again = jnp.exp(scores_of() - lse)
    d_probs = jnp.einsum(
        "sihe,sjhe->shij", d_mixed_heads, value_heads, preferred_element_type=single_float
    )
    centre = jnp.sum(probs_again * d_probs, axis=-1, keepdims=True)
    d_scores = (probs_again * (d_probs - centre)).astype(brain_float_half)
    d_query = (
        (
            jnp.einsum("shij,sjhe->sihe", d_scores, key_heads, preferred_element_type=single_float)
            * factor
        )
        .reshape(seqs, latent_rows, width_in)
        .astype(brain_float_half)
    )
    keys_gradient = (
        (
            jnp.einsum("shij,ihe->sjhe", d_scores, query_heads, preferred_element_type=single_float)
            * factor
        )
        .reshape(seqs, length, width_in)
        .astype(brain_float_half)
    )
    dq_total = jnp.sum(d_query.astype(single_float), axis=0)
    key_gradient_full = jnp.einsum(
        "vza,vzp->ap", input_normed_bf, keys_gradient, preferred_element_type=single_float
    )
    value_gradient_full = jnp.einsum(
        "vza,vzp->ap", input_normed_bf, values_gradient, preferred_element_type=single_float
    )
    input_norm_gradient = jnp.einsum(
        "yrz,kz->yrk", keys_gradient, key_projection, preferred_element_type=single_float
    ) + jnp.einsum(
        "yrz,kz->yrk", values_gradient, value_projection, preferred_element_type=single_float
    )
    d_inputs, grad_gin = norm_back(input_norm_gradient, in_unit, in_inv, g_in.astype(single_float))
    inputs_grad = d_inputs.astype(brain_float_half)
    residual_sum = jnp.sum(d_x_one, axis=0)
    mlp_sums = (
        lax.psum_scatter(grad_gmlp, "dp", scatter_dimension=0, tiled=True),
        lax.psum_scatter(grad_in, "dp", scatter_dimension=0, tiled=True),
        lax.psum_scatter(grad_back, "dp", scatter_dimension=0, tiled=True),
    )
    grad_query = jnp.dot(lat_b.astype(single_float).T, dq_total, precision=lax.Precision.HIGHEST)
    d_latnorm = jnp.dot(dq_total, w_query.astype(single_float).T, precision=lax.Precision.HIGHEST)
    d_base_part, grad_glat = norm_back(d_latnorm, lat_unit, lat_inv, g_lat.astype(single_float))
    attn_sums = (
        lax.psum_scatter(d_base_part + residual_sum, "dp", scatter_dimension=0, tiled=True),
        lax.psum_scatter(grad_glat, "dp", scatter_dimension=0, tiled=True),
        lax.psum_scatter(grad_query, "dp", scatter_dimension=0, tiled=True),
        lax.psum_scatter(grad_gin, "dp", scatter_dimension=0, tiled=True),
        lax.psum_scatter(key_gradient_full, "dp", scatter_dimension=0, tiled=True),
        lax.psum_scatter(value_gradient_full, "dp", scatter_dimension=0, tiled=True),
        lax.psum_scatter(grad_out, "dp", scatter_dimension=0, tiled=True),
    )
    base_grad, glat_grad, query_grad = (attn_sums[0], attn_sums[1], attn_sums[2])
    gin_grad, key_grad, value_grad, out_grad = (
        attn_sums[3],
        attn_sums[4],
        attn_sums[5],
        attn_sums[6],
    )
    return (
        latents,
        inputs_grad,
        base_grad,
        glat_grad,
        query_grad,
        gin_grad,
        key_grad,
        value_grad,
        out_grad,
        mlp_sums[0],
        mlp_sums[1],
        mlp_sums[2],
    )


def solution(mesh):
    in_specs = (
        P("dp", None, None),
        P("dp"),
        P("dp", None),
        P("dp", None, None),
        P("dp", None),
        P("dp"),
        P("dp", None),
        P("dp"),
        P("dp", None),
        P("dp", None),
        P("dp", None),
        P("dp"),
        P("dp", None),
        P("dp", None),
    )
    out_specs = (
        P("dp", None, None),
        P("dp", None, None),
        P("dp", None),
        P("dp"),
        P("dp", None),
        P("dp"),
        P("dp", None),
        P("dp", None),
        P("dp", None),
        P("dp"),
        P("dp", None),
        P("dp", None),
    )
    return jax.shard_map(local, mesh=mesh, in_specs=in_specs, out_specs=out_specs, check_vma=False)
```

profile of v0, /device:TPU:0, one launch (start us, length us, event | category | flops | bytes accessed | tf_op | source)
XLA Modules:
  0.0 1306.2 jit_solution(8882325805549450935)
XLA Ops:
  11.2 46.1 %all_gather.39 = bf16[256,1280]{1,0:T(8,128)(2,1)S(1)} all-gather(bf16[8,1280]{1,0:T(8,128)(2,1)} %param.18), channel_id=1, replica_groups=mesh['dp'=32] {'dp'}, dimensions={0}, use_global_device_ids=true | all-gather | bytes 675840 | tf_op jit(solution)/shard_map/all_gather | solution.py:56
  59.4 37.1 %all-reduce.7 = (bf16[768]{0:T(1024)(128)(2,1)S(1)}, bf16[1280]{0:T(1024)(128)(2,1)S(1)}, bf16[1280]{0:T(1024)(128)(2,1)S(1)}) all-reduce(bf16[768]{0:T(1024)(128)(2,1)S(1)} %dynamic-update-slice, bf16[1280]{0:T(1024)(128)(2,1)S(1)} %dynamic-update-slice.1, bf16[1280]{0:T(1024)(128)(2,1)S(1)} %dynamic-update-slice.2), channel_id=1, replica_groups=mesh['dp'=32] {'dp'}, use_global_device_ids=true, to_apply=%add | all-reduce | flops 3328 | bytes 13312
  111.9 9.7 convolution_convert_fusion
  133.8 48.3 %all-gather.11.cloned.1.call-done = bf16[1280,768]{1,0:T(8,128)(2,1)} async-done(((bf16[40,768]{1,0:T(8,128)(2,1)}), bf16[1280,768]{1,0:T(8,128)(2,1)}) %all-gather.11.cloned.1.call-update) | async-done | bytes 1966096 | tf_op jit(solution)/shard_map/all_gather | solution.py:58
  184.5 17.0 %bitcast_reduce_fusion = (f32[2,8,256]{2,0,1:T(2,128)S(1)}, f32[8,2,2048,256]{3,2,1,0:T(8,128)}) fusion(pred[2,2048]{1,0:T(4,128)(4,1)S(1)} %compare_and_fusion, bf16[256,8,96,1]{0,2,3,1:T(8,128)(2,1)S(1)} %bitcast.122, bf16[2,2048,8,96]{1,3,2,0:T(8,128)(2,1)} %bitcast.133), kind=kOutput, calls=%fused_computation.2 | convolution fusion | flops 1635774464 | bytes 40259584 | tf_op jit(solution)/shard_map/ihe,sjhe->shij/dot_general | solution.py:97
  201.6 15.1 %fusion.1 = f32[2,8,256]{2,0,1:T(2,128)S(1)} fusion(f32[8,2,2048,256]{3,2,1,0:T(8,128)} %get-tuple-element.68, f32[2,8,256]{2,0,1:T(2,128)S(1)} %get-tuple-element.67, pred[2,2048]{1,0:T(4,128)(4,1)S(1)} %compare_and_fusion), kind=kLoop, calls=%fused_computation.4 | loop fusion | flops 33550336 | bytes 33591296 | tf_op jit(solution)/shard_map/reduce_sum | solution.py:106
  231.4 11.4 fusion.64
  246.7 53.9 %all-gather.15.cloned.1.call-done = bf16[1280,1280]{1,0:T(8,128)(2,1)} async-done(((bf16[40,1280]{1,0:T(8,128)(2,1)}), bf16[1280,1280]{1,0:T(8,128)(2,1)}) %all-gather.15.cloned.1.call-update) | async-done | bytes 3276816 | tf_op jit(solution)/shard_map/all_gather | solution.py:66
  307.5 54.1 %all-gather.17.cloned.1.call-done = bf16[1280,1280]{1,0:T(8,128)(2,1)} async-done(((bf16[40,1280]{1,0:T(8,128)(2,1)}), bf16[1280,1280]{1,0:T(8,128)(2,1)}) %all-gather.17.cloned.1.call-update) | async-done | bytes 3276816 | tf_op jit(solution)/shard_map/all_gather | solution.py:67
  377.1 25.9 %multiply_reduce_fusion = (f32[2,8,256]{2,0,1:T(2,128)S(1)}, f32[2,8,256,2048]{2,3,0,1:T(8,128)}) fusion(f32[8,2,2048,256]{3,2,1,0:T(8,128)} %get-tuple-element.68, f32[2,8,256]{2,0,1:T(2,128)S(1)} %bitcast.129, pred[2,2048]{1,0:T(4,128)(4,1)S(1)} %compare_and_fusion, bf16[2,2048,8,96]{1,3,2,0:T(8,128)(2,1)} %bitcast.121, bf16[2,256,8,96]{1,3,2,0:T(8,128)(2,1)} %bitcast.116), kind=kOutput, calls=%fused_computation.7 | convolution fusion | flops 1652551680 | bytes 74223616 | tf_op jit(solution)/shard_map/sihe,sjhe->shij/dot_general | solution.py:159
  403.0 27.7 %multiply_convert_fusion = bf16[2,8,256,2048]{2,3,0,1:T(8,128)(2,1)} fusion(f32[2,8,256,2048]{2,3,0,1:T(8,128)} %get-tuple-element.74, f32[8,2,2048,256]{3,2,1,0:T(8,128)} %get-tuple-element.68, f32[2,8,256]{2,0,1:T(2,128)S(1)} %get-tuple-element.73, f32[2,8,256]{2,0,1:T(2,128)S(1)} %bitcast.130, pred[2,2048]{1,0:T(4,128)(4,1)S(1)} %compare_and_fusion), kind=kLoop, calls=%fused_computation.6 | loop fusion | flops 50331648 | bytes 83922944 | tf_op jit(solution)/shard_map/convert_element_type | solution.py:163
  430.7 10.4 convert_reduce_fusion.1
  448.3 10.9 fusion.28
  459.2 10.4 convolution_bitcast_fusion.3
  521.9 10.8 fusion.67
  532.8 15.1 %fusion.21 = (f32[768]{0:T(1024)S(1)}, f32[2,2048]{1,0:T(2,128)S(1)}, f32[2,2048]{1,0:T(2,128)S(1)}, f32[2,2048,768]{1,2,0:T(8,128)}) fusion(bf16[2,2048,768]{1,2,0:T(8,128)(2,1)S(1)} %bitcast.113, f32[2,2048]{1,0:T(2,128)S(1)} %add_rsqrt_fusion, f32[2,2048]{1,0:T(2,128)S(1)} %broadcast_multiply_fusion.2, f32[768]{0:T(1024)S(1)} %convert_element_type.104, ...), kind=kOutput, calls=%fused_computation.29 | convolution fusion | flops 4863286272 | bytes 39000064 | tf_op jit(solution)/shard_map/yrz,kz->yrk/dot_general | solution.py:189
  547.9 39.0 %all-reduce.6 = (f32[1280]{0:T(1024)S(1)}, f32[768]{0:T(1024)S(1)}, f32[1280]{0:T(1024)S(1)}) all-reduce(f32[1280]{0:T(1024)S(1)} %get-tuple-element.56, f32[768]{0:T(1024)S(1)} %get-tuple-element.48, f32[1280]{0:T(1024)S(1)} %get-tuple-element.51), channel_id=3, replica_groups=mesh['dp'=32] {'dp'}, use_global_device_ids=true, to_apply=%region_19.20.clone | all-reduce | flops 3328 | bytes 26624
  588.1 11.3 fusion.20
  614.2 70.3 %reduce-scatter.14.cloned.1.call-done = f32[24,768]{1,0:T(8,128)} async-done(((f32[768,768]{1,0:T(8,128)}), f32[24,768]{1,0:T(8,128)}) %reduce-scatter.14.cloned.1.call-update) | async-done | bytes 73744 | tf_op jit(solution)/shard_map/reduce_scatter | solution.py:209
  684.4 104.1 %reduce-scatter.12.cloned.1.call-done = f32[24,768]{1,0:T(8,128)} async-done(((f32[768,768]{1,0:T(8,128)}), f32[24,768]{1,0:T(8,128)}) %reduce-scatter.12.cloned.1.call-update) | async-done | bytes 73744 | tf_op jit(solution)/shard_map/reduce_scatter | solution.py:208
  788.5 109.9 %reduce-scatter.16.cloned.1.call-done = f32[24,1280]{1,0:T(8,128)} async-done(((f32[768,1280]{1,0:T(8,128)}), f32[24,1280]{1,0:T(8,128)}) %reduce-scatter.16.cloned.1.call-update) | async-done | bytes 122896 | tf_op jit(solution)/shard_map/reduce_scatter | solution.py:210
  898.4 109.8 %reduce-scatter.10.cloned.1.call-done = f32[40,768]{1,0:T(8,128)} async-done(((f32[1280,768]{1,0:T(8,128)}), f32[40,768]{1,0:T(8,128)}) %reduce-scatter.10.cloned.1.call-update) | async-done | bytes 122896 | tf_op jit(solution)/shard_map/reduce_scatter | solution.py:206
  1008.3 147.1 %reduce-scatter.18.cloned.1.call-done = f32[40,1280]{1,0:T(8,128)} async-done(((f32[1280,1280]{1,0:T(8,128)}), f32[40,1280]{1,0:T(8,128)}) %reduce-scatter.18.cloned.1.call-update) | async-done | bytes 204816 | tf_op jit(solution)/shard_map/reduce_scatter | solution.py:197
  1155.3 144.1 %reduce-scatter.20.cloned.1.call-done = f32[40,1280]{1,0:T(8,128)} async-done(((f32[1280,1280]{1,0:T(8,128)}), f32[40,1280]{1,0:T(8,128)}) %reduce-scatter.20.cloned.1.call-update) | async-done | bytes 204816 | tf_op jit(solution)/shard_map/reduce_scatter | solution.py:198
  (140 shorter events, 152.1 us)
Async XLA Ops:
  7.2 51.5 %copy-start.21 = (bf16[40]{0:T(256)(128)(2,1)S(1)}, bf16[40]{0:T(256)(128)(2,1)}, u32[]{:S(2)}) copy-start(bf16[40]{0:T(256)(128)(2,1)} %param.19) | copy-start | bytes 244
  7.2 51.7 %copy-start.22 = (bf16[40]{0:T(256)(128)(2,1)S(1)}, bf16[40]{0:T(256)(128)(2,1)}, u32[]{:S(2)}) copy-start(bf16[40]{0:T(256)(128)(2,1)} %param.25) | copy-start | bytes 244
  7.2 51.9 %copy-start.23 = (bf16[24]{0:T(256)(128)(2,1)S(1)}, bf16[24]{0:T(256)(128)(2,1)}, u32[]{:S(2)}) copy-start(bf16[24]{0:T(256)(128)(2,1)} %param.21) | copy-start | bytes 148
  7.2 104.7 %all-gather.9.cloned.1.call-start = ((), (), s32[]{:S(2)}) async-start(), calls=%async_computation.8 | async-start | bytes 1216512 | tf_op jit(solution)/shard_map/all_gather | solution.py:60
  7.9 116.2 %all-gather.7.cloned.1.call-start = ((), (), s32[]{:S(2)}) async-start(), calls=%async_computation.7 | async-start | bytes 1216512 | tf_op jit(solution)/shard_map/all_gather | solution.py:61
  8.7 173.4 %all-gather.11.cloned.1.call-start = ((), (), s32[]{:S(2)}) async-start(), calls=%async_computation.9 | async-start | bytes 2027520 | tf_op jit(solution)/shard_map/all_gather | solution.py:58
  9.4 233.4 %all-gather.13.cloned.1.call-start = ((), (), s32[]{:S(2)}) async-start(), calls=%async_computation.10 | async-start | bytes 2027520 | tf_op jit(solution)/shard_map/all_gather | solution.py:62
  10.0 290.6 %all-gather.15.cloned.1.call-start = ((), (), s32[]{:S(2)}) async-start(), calls=%async_computation.11 | async-start | bytes 3379200 | tf_op jit(solution)/shard_map/all_gather | solution.py:66
  10.6 350.9 %all-gather.17.cloned.1.call-start = ((), (), s32[]{:S(2)}) async-start(), calls=%async_computation.12 | async-start | bytes 3379200 | tf_op jit(solution)/shard_map/all_gather | solution.py:67
  11.2 603.0 %reduce-scatter.8.cloned.1.call-start = ((), (), s32[]{:S(2)}) async-start(), calls=%async_computation.13 | async-start | bytes 1351680 | tf_op jit(solution)/shard_map/reduce_scatter | solution.py:204
  184.5 17.1 %copy-start.8 = (bf16[256,768]{0,1:T(8,128)(2,1)}, bf16[256,768]{0,1:T(8,128)(2,1)S(1)}, u32[]{:S(2)}) copy-start(bf16[256,768]{0,1:T(8,128)(2,1)S(1)} %copy.70) | copy-start | bytes 1179652
  201.6 20.3 %copy-start = (f32[8,2,2048,256]{3,2,1,0:T(8,128)S(1)}, f32[8,2,2048,256]{3,2,1,0:T(8,128)}, u32[]{:S(2)}) copy-start(f32[8,2,2048,256]{3,2,1,0:T(8,128)} %get-tuple-element.68) | copy-start | bytes 100663296
  246.3 254.7 %copy-start.2 = (f32[2,256,1280]{2,1,0:T(8,128)}, f32[2,256,1280]{2,1,0:T(8,128)S(1)}, u32[]{:S(2)}) copy-start(f32[2,256,1280]{2,1,0:T(8,128)S(1)} %get-tuple-element.70) | copy-start | bytes 7864324
  448.3 236.2 %reduce-scatter.14.cloned.1.call-start = ((), (), s32[]{:S(2)}) async-start(), calls=%async_computation.16 | async-start | bytes 2433024 | tf_op jit(solution)/shard_map/reduce_scatter | solution.py:209
  469.6 318.9 %reduce-scatter.12.cloned.1.call-start = ((), (), s32[]{:S(2)}) async-start(), calls=%async_computation.15 | async-start | bytes 2433024 | tf_op jit(solution)/shard_map/reduce_scatter | solution.py:208
  490.6 407.8 %reduce-scatter.16.cloned.1.call-start = ((), (), s32[]{:S(2)}) async-start(), calls=%async_computation.17 | async-start | bytes 4055040 | tf_op jit(solution)/shard_map/reduce_scatter | solution.py:210
  495.3 512.9 %reduce-scatter.10.cloned.1.call-start = ((), (), s32[]{:S(2)}) async-start(), calls=%async_computation.14 | async-start | bytes 4055040 | tf_op jit(solution)/shard_map/reduce_scatter | solution.py:206
  500.9 654.4 %reduce-scatter.18.cloned.1.call-start = ((), (), s32[]{:S(2)}) async-start(), calls=%async_computation.18 | async-start | bytes 6758400 | tf_op jit(solution)/shard_map/reduce_scatter | solution.py:197
  507.1 792.4 %reduce-scatter.20.cloned.1.call-start = ((), (), s32[]{:S(2)}) async-start(), calls=%async_computation.19 | async-start | bytes 6758400 | tf_op jit(solution)/shard_map/reduce_scatter | solution.py:198
  507.1 8.9 copy-start.10
  520.7 12.1 slice-start
  521.9 10.8 slice-start.1
  521.9 10.8 copy-start.20
  599.5 9.4 copy-start.3
  (16 other events, 44.2 us)
Sparse Core Ops, SparseCore 0:
  10.9 57.2 all-gather.8
  71.1 52.9 all-gather.6
  127.0 55.0 all-gather.10
  184.8 54.9 all-gather.12
  242.5 58.0 all-gather.14
  303.4 58.1 all-gather.16
  448.4 134.4 reduce-scatter.7
  589.6 94.8 reduce-scatter.13
  690.3 98.1 reduce-scatter.11
  795.2 103.1 reduce-scatter.15
  905.3 102.9 reduce-scatter.9
  1011.1 144.1 reduce-scatter.17
  1158.3 141.1 reduce-scatter.19
where the time goes:
time: 1320 us; the launch traced here: 1310 us
  waiting for transfers between devices  848 us (64%)
  matrix products  203 us (15%)
  blocking collectives  122 us (9%)
  other arithmetic  81.4 us (6%)
  local copies, waits for them, and re-layouts  36.4 us (3%)
  between operations  14.5 us (1%)
    reduce_scatter x1, waiting for transfers between devices, local(): lax.psum_scatter(grad_in, 'dp', scatter_dimension=0, tiled=True)  147 us
    reduce_scatter x1, waiting for transfers between devices, local(): lax.psum_scatter(grad_back, 'dp', scatter_dimension=0, tiled=True)  144 us
    reduce_scatter x1, waiting for transfers between devices, local(): lax.psum_scatter(grad_out, 'dp', scatter_dimension=0, tiled=True)  110 us
    reduce_scatter x1, waiting for transfers between devices, local(): lax.psum_scatter(grad_query, 'dp', scatter_dimension=0, tiled=True)  110 us
    reduce_scatter x1, waiting for transfers between devices, local(): lax.psum_scatter(key_gradient_full, 'dp', scatter_dimension=0, tiled=True)  104 us
    unnamed x2, blocking collectives  76.2 us
    reduce_scatter x1, waiting for transfers between devices, local(): lax.psum_scatter(value_gradient_full, 'dp', scatter_dimension=0, tiled=True)  70.3 us
    all_gather x1, waiting for transfers between devices, local(): lax.all_gather(mlp_out_weight, 'dp', axis=0, tiled=True)  54.1 us
  transfers between devices with their start and end apart: 13, of which 10 were waited for; matrix products, arithmetic and copies ran while one was open for 17% of the time, Pallas kernels for 0%

commit v1 on v0

v1 whole, which is shorter than its diff:
```python
import functools
import math

import jax
import jax.numpy as jnp
from jax import lax
from jax.experimental import pallas as pl
from jax.experimental.pallas import tpu as pltpu
from jax.sharding import PartitionSpec as P

HEADS = 8
HEAD = 96
PADDED = 112
MASKED = -1e30
VMEM = 56 * 1024 * 1024
F32 = jnp.float32
BF16 = jnp.bfloat16


def nn(a, b):
    return lax.dot_general(a, b, (((1,), (0,)), ((), ())), preferred_element_type=F32)


def nt(a, b):
    return lax.dot_general(a, b, (((1,), (1,)), ((), ())), preferred_element_type=F32)


def tn(a, b):
    return lax.dot_general(a, b, (((0,), (0,)), ((), ())), preferred_element_type=F32)


def unit_rows(rows):
    centred = rows - jnp.mean(rows, axis=-1, keepdims=True)
    inverse = lax.rsqrt(jnp.mean(centred * centred, axis=-1, keepdims=True) + 1e-05)
    return centred * inverse, inverse


def norm_back(upstream, unit, inverse, gain):
    scaled = upstream * gain
    inner = (
        scaled
        - jnp.mean(scaled, axis=-1, keepdims=True)
        - unit * jnp.mean(scaled * unit, axis=-1, keepdims=True)
    )
    return inverse * inner


def gelu_slope(value_rows):
    cdf = 0.5 * (1.0 + jax.scipy.special.erf(value_rows * (1.0 / math.sqrt(2.0))))
    return cdf + value_rows * jnp.exp(-0.5 * value_rows * value_rows) * (
        1.0 / math.sqrt(2.0 * math.pi)
    )


def grid_of(devices):
    known = {32: (4, 2, 2, 2), 128: (4, 4, 4, 2)}
    if devices in known:
        return known[devices]
    dims, left = [], devices
    while left > 1:
        step = next(f for f in (2, 3, 4, 5, 7, left) if left % f == 0)
        dims.insert(0, step)
        left //= step
    return tuple(dims)


class Grid:
    def __init__(self, devices):
        self.devices = devices
        self.dims = grid_of(devices)
        self.strides = tuple(math.prod(self.dims[i + 1 :]) for i in range(len(self.dims)))
        me = lax.axis_index("dp")
        self.mine = tuple((me // s) % k for s, k in zip(self.strides, self.dims))
        last = len(self.dims) - 1
        near = list(range(1, last))
        self.order_a = (0, *near[::-1], last) if last else (0,)
        self.order_b = (0, *near, last) if last else (0,)

    def shift(self, dim, r):
        k, s = self.dims[dim], self.strides[dim]
        pairs = []
        for i in range(self.devices):
            at = (i // s) % k
            pairs.append((i, i + (((at + r) % k) - at) * s))
        return pairs

    def gather(self, block, order):
        stack = block[None]
        for dim in order:
            k = self.dims[dim]
            parts = [stack]
            for r in range(1, k):
                parts.append(lax.ppermute(stack, "dp", self.shift(dim, k - r)))
            stack = jnp.concatenate(parts, axis=0)
        return stack

    def found(self, order):
        sizes = [self.dims[dim] for dim in order]
        index = jnp.zeros((1,) * len(self.dims), jnp.int32)
        for n, dim in enumerate(order):
            step = math.prod(sizes[:n])
            away = (jnp.arange(self.dims[dim], dtype=jnp.int32) - self.mine[dim]) % self.dims[dim]
            shape = [1] * len(self.dims)
            shape[dim] = self.dims[dim]
            index = index + (away * step).reshape(shape)
        return index.reshape(-1)

    def scatter_sum(self, whole, order):
        rest = list(range(len(self.dims)))
        wire = whole.dtype
        value = whole.reshape(*self.dims, *whole.shape[1:])
        for dim in order:
            axis = rest.index(dim)
            k, me = self.dims[dim], self.mine[dim]

            def take(at):
                return lax.dynamic_index_in_dim(value, at, axis, keepdims=False)

            total = take(me).astype(F32)
            for r in range(1, k):
                sent = take((me + r) % k)
                total = total + lax.ppermute(sent, "dp", self.shift(dim, r)).astype(F32)
            rest.pop(axis)
            value = total if not rest else total.astype(wire)
        return value


def prepare_kernel(
    cuts, place_ref, a_ref, b_ref, wt_ref, wq_ref, lat_ref, q_ref, qt_ref, gin_ref, glat_ref, gmlp_ref, kv_ref
):
    devices, width = a_ref.shape[0], a_ref.shape[2]
    k_rows, q_top, q_low, l_rows, l_width = cuts
    q_rows = q_top + q_low
    lines = []
    for d in range(devices):
        a = a_ref.at[place_ref[0, d]]
        b = b_ref.at[place_ref[1, d]]
        kv_ref[d * k_rows : (d + 1) * k_rows, :width] = a[:k_rows]
        kv_ref[d * k_rows : (d + 1) * k_rows, width:] = b[:k_rows]
        wq_ref[d * q_rows : d * q_rows + q_top] = a[k_rows : k_rows + q_top]
        at = k_rows + q_low
        wq_ref[d * q_rows + q_top : (d + 1) * q_rows] = b[k_rows:at]
        lat_ref[d * l_rows : (d + 1) * l_rows, :width] = b[at : at + l_rows]
        spare = b[at + l_rows : at + 2 * l_rows]
        lat_ref[d * l_rows : (d + 1) * l_rows, width:] = spare[:, : l_width - width]
        lines.append(spare[:1, l_width - width :].astype(F32))
    first = 0
    for ref, size in ((gin_ref, k_rows), (glat_ref, q_rows), (gmlp_ref, q_rows)):
        ref[...] = jnp.concatenate([line[:, first : first + size] for line in lines], axis=1)
        first += size
    for c in range(0, wt_ref.shape[0], width):
        wt_ref[c : c + width] = kv_ref[:, c : c + width].T
    unit, _ = unit_rows(lat_ref[...].astype(F32))
    query = nn((unit * glat_ref[...]).astype(BF16), wq_ref[...])
    qt_ref[...] = query.T.astype(BF16)
    query = query.astype(BF16)
    column = lax.broadcasted_iota(jnp.int32, (query.shape[0], PADDED - HEAD), 1)
    ones = jnp.where(column == 0, 1.0, 0.0).astype(BF16)
    for h in range(HEADS):
        q_ref[h] = jnp.concatenate([query[:, h * HEAD : (h + 1) * HEAD], ones], axis=1)


def prepare(stack_a, stack_b, places, cuts):
    devices, _, width = stack_a.shape
    k_rows, q_top, q_low, l_rows, l_width = cuts
    rows = devices * l_rows
    vmem = pl.BlockSpec(memory_space=pltpu.VMEM)
    shapes = [
        ((2 * width, width), BF16),
        ((devices * (q_top + q_low), width), BF16),
        ((rows, l_width), BF16),
        ((HEADS, rows, PADDED), BF16),
        ((width, rows), BF16),
        ((1, width), F32),
        ((1, l_width), F32),
        ((1, l_width), F32),
    ]
    return pl.pallas_call(
        functools.partial(prepare_kernel, cuts),
        in_specs=[pl.BlockSpec(memory_space=pltpu.SMEM), vmem, vmem],
        out_specs=[vmem] * len(shapes),
        out_shape=[jax.ShapeDtypeStruct(*s) for s in shapes],
        scratch_shapes=[pltpu.VMEM((width, 2 * width), BF16)],
        compiler_params=pltpu.CompilerParams(vmem_limit_bytes=VMEM),
        name="prepare",
    )(places, stack_a, stack_b)


def project_kernel(x_ref, gain_ref, w_ref, addend_ref, normed_ref, k_ref, v_ref):
    unit, _ = unit_rows(x_ref[0].astype(F32))
    normed = (unit * gain_ref[...]).astype(BF16)
    normed_ref[0] = normed
    slots = normed.shape[0]
    both = nt(w_ref[...], normed).astype(BF16)
    row = lax.broadcasted_iota(jnp.int32, (PADDED - HEAD, slots), 0)
    mask_rows = jnp.where(row == 0, jnp.broadcast_to(addend_ref[0], row.shape), 0.0).astype(BF16)
    one_rows = jnp.where(row < 3, 1.0, 0.0).astype(BF16)
    for h in range(HEADS):
        k_ref[0, h, :HEAD] = both[h * HEAD : (h + 1) * HEAD]
        k_ref[0, h, HEAD:] = mask_rows
        v_ref[0, h, :HEAD] = both[(HEADS + h) * HEAD : (HEADS + h + 1) * HEAD]
        v_ref[0, h, HEAD:] = one_rows


def project(x, gain, weights, addend, tile=512):
    seqs, slots, width = x.shape
    rows = pl.BlockSpec((1, tile, width), lambda s, j: (s, j, 0))
    heads = pl.BlockSpec((1, HEADS, PADDED, tile), lambda s, j: (s, 0, 0, j))
    whole = lambda a: pl.BlockSpec(a.shape, lambda s, j: (0,) * a.ndim)
    return pl.pallas_call(
        project_kernel,
        grid=(seqs, slots // tile),
        in_specs=[rows, whole(gain), whole(weights), pl.BlockSpec((1, 1, tile), lambda s, j: (s, 0, j))],
        out_specs=[rows, heads, heads],
        out_shape=[
            jax.ShapeDtypeStruct(x.shape, BF16),
            jax.ShapeDtypeStruct((seqs, HEADS, PADDED, slots), BF16),
            jax.ShapeDtypeStruct((seqs, HEADS, PADDED, slots), BF16),
        ],
        compiler_params=pltpu.CompilerParams(vmem_limit_bytes=VMEM),
        cost_estimate=pl.CostEstimate(
            flops=4 * seqs * slots * width * width, bytes_accessed=10 * seqs * slots * width, transcendentals=0
        ),
        name="project",
    )(x, gain, weights, addend)


def attend_kernel(chunk, scale, q_ref, k_ref, v_ref, mixed_ref, log_ref, score_ref):
    slots = k_ref.shape[-1]
    outs, logs = [], []
    for h in range(q_ref.shape[0]):
        score = score_ref.at[h % 2]
        top = None
        for j in range(0, slots, chunk):
            piece = nn(q_ref[h], k_ref[0, h, :, j : j + chunk])
            score[:, j : j + chunk] = piece
            for t in range(0, chunk, 128):
                part = piece[:, t : t + 128]
                top = part if top is None else jnp.maximum(top, part)
        top = jnp.max(top, axis=-1, keepdims=True)
        total = None
        for j in range(0, slots, chunk):
            power = jnp.exp2((score[:, j : j + chunk] - top) * scale).astype(BF16)
            piece = nt(power, v_ref[0, h, :, j : j + chunk])
            total = piece if total is None else total + piece
        weight = total[:, HEAD : HEAD + 1]
        outs.append(total[:, :HEAD] / weight)
        logs.append(top * scale + jnp.log2(weight))
    mixed_ref[0] = jnp.concatenate(outs, axis=1)
    for h, log in enumerate(logs):
        log_ref[0, h] = jnp.broadcast_to(log, log_ref.shape[2:])


def attend(q, k, v, chunk=1024, group=4):
    seqs, _, _, slots = k.shape
    rows = q.shape[1]
    scale = math.log2(math.e) / math.sqrt(HEAD)
    heads = pl.BlockSpec((1, group, PADDED, slots), lambda s, g: (s, g, 0, 0))
    return pl.pallas_call(
        functools.partial(attend_kernel, chunk, scale),
        grid=(seqs, HEADS // group),
        in_specs=[pl.BlockSpec((group, rows, PADDED), lambda s, g: (g, 0, 0)), heads, heads],
        out_specs=[
            pl.BlockSpec((1, rows, group * HEAD), lambda s, g: (s, 0, g)),
            pl.BlockSpec((1, group, rows, 128), lambda s, g: (s, g, 0, 0)),
        ],
        out_shape=[
            jax.ShapeDtypeStruct((seqs, rows, HEADS * HEAD), F32),
            jax.ShapeDtypeStruct((seqs, HEADS, rows, 128), F32),
        ],
        scratch_shapes=[pltpu.VMEM((2, rows, slots), F32)],
        compiler_params=pltpu.CompilerParams(vmem_limit_bytes=VMEM),
        cost_estimate=pl.CostEstimate(
            flops=16 * seqs * rows * slots * HEADS * HEAD,
            bytes_accessed=4 * seqs * HEADS * PADDED * slots,
            transcendentals=seqs * HEADS * rows * slots,
        ),
        name="attend",
    )(q, k, v)


def attend_back_kernel(
    chunk, scale, factor, q_ref, qt_ref, k_ref, v_ref, log_ref, dm_ref, dmt_ref, dq_ref, dk_ref, dv_ref
):
    slots = k_ref.shape[-1]
    grads = []
    for h in range(q_ref.shape[0]):
        log = log_ref[0, h][:, :1]
        mine = slice(h * HEAD, (h + 1) * HEAD)
        total = None
        for j in range(0, slots, chunk):
            keys = k_ref[0, h, :, j : j + chunk]
            probs = jnp.exp2(nn(q_ref[h], keys) * scale - log)
            less = nn(dm_ref[0, h], v_ref[0, h, :, j : j + chunk])
            d_scores = (probs * less).astype(BF16)
            dv_ref[0, mine, j : j + chunk] = nn(dmt_ref[0, mine], probs.astype(BF16)).astype(BF16)
            dk_ref[0, mine, j : j + chunk] = (nn(qt_ref[mine], d_scores) * factor).astype(BF16)
            piece = nt(d_scores, keys[:HEAD])
            total = piece if total is None else total + piece
        grads.append((total * factor).astype(BF16))
    dq_ref[0] = jnp.concatenate(grads, axis=1)


def attend_back(q, qt, k, v, log, dm, dmt, chunk=2048, group=4):
    seqs, _, _, slots = k.shape
    rows = q.shape[1]
    scale = math.log2(math.e) / math.sqrt(HEAD)
    heads = pl.BlockSpec((1, group, PADDED, slots), lambda s, g: (s, g, 0, 0))
    features = pl.BlockSpec((1, group * HEAD, slots), lambda s, g: (s, g, 0))
    return pl.pallas_call(
        functools.partial(attend_back_kernel, chunk, scale, 1.0 / math.sqrt(HEAD)),
        grid=(seqs, HEADS // group),
        in_specs=[
            pl.BlockSpec((group, rows, PADDED), lambda s, g: (g, 0, 0)),
            pl.BlockSpec((group * HEAD, rows), lambda s, g: (g, 0)),
            heads,
            heads,
            pl.BlockSpec((1, group, rows, 128), lambda s, g: (s, g, 0, 0)),
            pl.BlockSpec((1, group, rows, PADDED), lambda s, g: (s, g, 0, 0)),
            pl.BlockSpec((1, group * HEAD, rows), lambda s, g: (s, g, 0)),
        ],
        out_specs=[pl.BlockSpec((1, rows, group * HEAD), lambda s, g: (s, 0, g)), features, features],
        out_shape=[
            jax.ShapeDtypeStruct((seqs, rows, HEADS * HEAD), BF16),
            jax.ShapeDtypeStruct((seqs, HEADS * HEAD, slots), BF16),
            jax.ShapeDtypeStruct((seqs, HEADS * HEAD, slots), BF16),
        ],
        compiler_params=pltpu.CompilerParams(vmem_limit_bytes=VMEM),
        cost_estimate=pl.CostEstimate(
            flops=40 * seqs * rows * slots * HEADS * HEAD,
            bytes_accessed=8 * seqs * HEADS * PADDED * slots,
            transcendentals=seqs * HEADS * rows * slots,
        ),
        name="attend_back",
    )(q, qt, k, v, log, dm, dmt)


def kv_grad_kernel(dk_ref, dv_ref, normed_ref, gk_ref, gv_ref, total_ref):
    step = pl.program_id(0) * pl.num_programs(1) + pl.program_id(1)
    normed = normed_ref[0]
    for n, ref in enumerate((dk_ref, dv_ref)):
        piece = nn(ref[0], normed)

        @pl.when(step == 0)
        def _():
            total_ref[n] = piece

        @pl.when(step > 0)
        def _():
            total_ref[n] += piece

    @pl.when(step == pl.num_programs(0) * pl.num_programs(1) - 1)
    def _():
        gk_ref[...] = total_ref[0].T.astype(BF16)
        gv_ref[...] = total_ref[1].T.astype(BF16)


def kv_grad(dk, dv, normed, tile=1024):
    seqs, features, slots = dk.shape
    width = normed.shape[-1]
    columns = pl.BlockSpec((1, features, tile), lambda s, j: (s, 0, j))
    whole = pl.BlockSpec((width, features), lambda s, j: (0, 0))
    return pl.pallas_call(
        kv_grad_kernel,
        grid=(seqs, slots // tile),
        in_specs=[columns, columns, pl.BlockSpec((1, tile, width), lambda s, j: (s, j, 0))],
        out_specs=[whole, whole],
        out_shape=[jax.ShapeDtypeStruct((width, features), BF16)] * 2,
        scratch_shapes=[pltpu.VMEM((2, features, width), F32)],
        compiler_params=pltpu.CompilerParams(vmem_limit_bytes=VMEM),
        cost_estimate=pl.CostEstimate(
            flops=4 * seqs * slots * width * features, bytes_accessed=6 * seqs * slots * width, transcendentals=0
        ),
        name="kv_grad",
    )(dk, dv, normed)


def input_grad_kernel(dk_ref, dv_ref, w_ref, gain_ref, x_ref, out_ref):
    features = dk_ref.shape[1]
    upstream = tn(dk_ref[0], w_ref[:features]) + tn(dv_ref[0], w_ref[features:])
    unit, inverse = unit_rows(x_ref[0].astype(F32))
    out_ref[0] = norm_back(upstream, unit, inverse, gain_ref[...]).astype(BF16)


def input_grad(dk, dv, weights, gain, x, tile=512):
    seqs, features, slots = dk.shape
    width = x.shape[-1]
    columns = pl.BlockSpec((1, features, tile), lambda s, j: (s, 0, j))
    rows = pl.BlockSpec((1, tile, width), lambda s, j: (s, j, 0))
    whole = lambda a: pl.BlockSpec(a.shape, lambda s, j: (0,) * a.ndim)
    return pl.pallas_call(
        input_grad_kernel,
        grid=(seqs, slots // tile),
        in_specs=[columns, columns, whole(weights), whole(gain), rows],
        out_specs=rows,
        out_shape=jax.ShapeDtypeStruct(x.shape, BF16),
        compiler_params=pltpu.CompilerParams(vmem_limit_bytes=VMEM),
        cost_estimate=pl.CostEstimate(
            flops=4 * seqs * slots * width * features, bytes_accessed=8 * seqs * slots * width, transcendentals=0
        ),
        name="input_grad",
    )(dk, dv, weights, gain, x)


def local(
    byte_inputs,
    lengths,
    key_mask,
    latents_cot,
    latent_array,
    lat_gain,
    query_weight,
    in_gain,
    key_weight,
    value_weight,
    out_weight,
    mlp_gain,
    mlp_in_weight,
    mlp_out_weight,
):
    devices = lax.axis_size("dp")
    grid = Grid(devices)
    seqs, length, width = byte_inputs.shape
    k_rows, q_rows, l_rows = key_weight.shape[0], query_weight.shape[0], latent_array.shape[0]
    l_width = latent_array.shape[1]
    rows = devices * l_rows
    q_top = k_rows if q_rows > k_rows else q_rows // 2
    q_low = q_rows - q_top
    cuts = (k_rows, q_top, q_low, l_rows, l_width)

    late = lax.all_gather(jnp.concatenate([out_weight, mlp_in_weight, mlp_out_weight], axis=0), "dp")

    gains = jnp.concatenate([in_gain, lat_gain, mlp_gain])
    spare = 2 * width - l_width
    gain_rows = jnp.broadcast_to(jnp.pad(gains, (0, spare - gains.shape[0])), (l_rows, spare))
    block_a = jnp.concatenate([key_weight, query_weight[:q_top]], axis=0)
    block_b = jnp.concatenate(
        [
            value_weight,
            query_weight[q_top:],
            latent_array[:, :width],
            jnp.concatenate([latent_array[:, width:], gain_rows], axis=1),
        ],
        axis=0,
    )
    stack_a = grid.gather(block_a, grid.order_a)
    stack_b = grid.gather(block_b, grid.order_b)
    places = jnp.stack([grid.found(grid.order_a), grid.found(grid.order_b)])
    kv_weights, w_query, base, q, qt, g_in, g_lat, g_mlp = prepare(stack_a, stack_b, places, cuts)

    positions = jnp.arange(length, dtype=jnp.int32)
    valid = (positions[None, :] < lengths[:, None]) & (key_mask == 1)
    addend = jnp.where(valid, 0.0, MASKED).astype(F32)[:, None]
    normed, k, v = project(byte_inputs, g_in, kv_weights, addend)
    mixed32, log = attend(q, k, v)

    w_out = late[:, :k_rows].reshape(-1, l_width)
    w_in = late[:, k_rows : k_rows + q_rows].reshape(-1, l_width)
    w_back = late[:, k_rows + q_rows :].reshape(-1, l_width)
    base32 = base.astype(F32)
    lat_unit, lat_inv = unit_rows(base32)
    lat_b = (lat_unit * g_lat).astype(BF16)
    mixed = mixed32.astype(BF16)
    x_one = base32[None] + jnp.einsum("sie,ef->sif", mixed, w_out, preferred_element_type=F32)
    mlp_unit, mlp_inv = unit_rows(x_one)
    mlp_b = (mlp_unit * g_mlp).astype(BF16)
    pre = jnp.einsum("sid,dh->sih", mlp_b, w_in, preferred_element_type=F32)
    act = jax.nn.gelu(pre, approximate=False).astype(BF16)
    latents = (
        x_one + jnp.einsum("sih,hf->sif", act, w_back, preferred_element_type=F32)
    ).astype(BF16)

    cot32 = latents_cot.astype(F32)
    d_act = jnp.einsum("sif,hf->sih", latents_cot, w_back, preferred_element_type=F32)
    d_pre = (d_act * gelu_slope(pre)).astype(BF16)
    d_mlpnorm = jnp.einsum("sih,dh->sid", d_pre, w_in, preferred_element_type=F32)
    d_x_one = cot32 + norm_back(d_mlpnorm, mlp_unit, mlp_inv, g_mlp)
    d_attn = d_x_one.astype(BF16)
    d_mixed = jnp.einsum("sif,ef->sie", d_attn, w_out, preferred_element_type=F32).astype(BF16)
    grad_back = jnp.einsum("sih,sif->hf", act, latents_cot, preferred_element_type=F32)
    grad_in = jnp.einsum("sid,sih->dh", mlp_b, d_pre, preferred_element_type=F32)
    grad_out = jnp.einsum("sie,sif->ef", mixed, d_attn, preferred_element_type=F32)

    def blocks(g):
        return g.astype(BF16).reshape(devices, g.shape[0] // devices, g.shape[1])

    back_order_a, back_order_b = grid.order_a[::-1], grid.order_b[::-1]
    in_grad = grid.scatter_sum(blocks(grad_in), back_order_a)
    back_grad = grid.scatter_sum(blocks(grad_back), back_order_b)
    out_grad = lax.psum_scatter(grad_out, "dp", scatter_dimension=0, tiled=True)

    dm_heads = d_mixed.reshape(seqs, rows, HEADS, HEAD).transpose(0, 2, 1, 3)
    mixed_heads = mixed32.reshape(seqs, rows, HEADS, HEAD).transpose(0, 2, 1, 3)
    centre = -jnp.sum(dm_heads.astype(F32) * mixed_heads, axis=-1, keepdims=True)
    high = lax.reduce_precision(centre, 8, 7)
    middle = lax.reduce_precision(centre - high, 8, 7)
    low = centre - high - middle
    pieces = [dm_heads] + [p.astype(BF16) for p in (high, middle, low)]
    pieces.append(jnp.zeros((seqs, HEADS, rows, PADDED - HEAD - 3), BF16))
    dm = jnp.concatenate(pieces, axis=-1)
    d_query, dk, dv = attend_back(q, qt, k, v, log, dm, d_mixed.transpose(0, 2, 1))

    grad_query = jnp.einsum("ic,sia->ca", lat_b, d_query, preferred_element_type=F32)
    d_latnorm = jnp.einsum("sia,ca->ic", d_query, w_query, preferred_element_type=F32)
    base_local = norm_back(d_latnorm, lat_unit, lat_inv, g_lat) + jnp.sum(d_x_one, axis=0)
    query_blocks, base_blocks = blocks(grad_query), blocks(base_local)
    room = jnp.zeros((devices, l_rows, spare), BF16)
    sum_a = grid.scatter_sum(query_blocks[:, :q_top], back_order_a)
    sum_b = grid.scatter_sum(
        jnp.concatenate(
            [
                query_blocks[:, q_top:],
                base_blocks[:, :, :width],
                jnp.concatenate([base_blocks[:, :, width:], room], axis=2),
            ],
            axis=1,
        ),
        back_order_b,
    )
    query_grad = jnp.concatenate([sum_a, sum_b[:q_low]], axis=0)
    base_grad = jnp.concatenate(
        [sum_b[q_low : q_low + l_rows], sum_b[q_low + l_rows :, : l_width - width]], axis=1
    )

    grad_key, grad_value = kv_grad(dk, dv, normed)
    key_grad = grid.scatter_sum(blocks(grad_key), back_order_a)
    value_grad = grid.scatter_sum(blocks(grad_value), back_order_b)
    inputs_grad = input_grad(dk, dv, kv_weights, g_in, byte_inputs)

    def gain_grad(gain, *pairs):
        total = sum(jnp.sum(g * w.astype(F32), axis=1) for g, w in pairs)
        return total / gain.astype(F32)

    gin_grad = gain_grad(in_gain, (key_grad, key_weight), (value_grad, value_weight))
    glat_grad = gain_grad(lat_gain, (query_grad, query_weight))
    gmlp_grad = gain_grad(mlp_gain, (in_grad, mlp_in_weight))
    return (
        latents,
        inputs_grad,
        base_grad,
        glat_grad,
        query_grad,
        gin_grad,
        key_grad,
        value_grad,
        out_grad,
        gmlp_grad,
        in_grad,
        back_grad,
    )


def solution(mesh):
    in_specs = (
        P("dp", None, None),
        P("dp"),
        P("dp", None),
        P("dp", None, None),
        P("dp", None),
        P("dp"),
        P("dp", None),
        P("dp"),
        P("dp", None),
        P("dp", None),
        P("dp", None),
        P("dp"),
        P("dp", None),
        P("dp", None),
    )
    out_specs = (
        P("dp", None, None),
        P("dp", None, None),
        P("dp", None),
        P("dp"),
        P("dp", None),
        P("dp"),
        P("dp", None),
        P("dp", None),
        P("dp", None),
        P("dp"),
        P("dp", None),
        P("dp", None),
    )
    return jax.shard_map(local, mesh=mesh, in_specs=in_specs, out_specs=out_specs, check_vma=False)
```

time: 1320 us -> 396 us (0.30)
  waiting for transfers between devices: 848 us -> 74.3 us
  matrix products: 203 us -> 27 us
  blocking collectives: 122 us -> 0 us
  Pallas kernels: 0 us -> 105 us
  starting transfers between devices: 0.92 us -> 67 us
  other arithmetic: 81.4 us -> 45 us
  local copies, waits for them, and re-layouts: 36.4 us -> 56.7 us
    reduce_scatter x7 -> x1, waiting for transfers between devices: 685 us -> 0.4 us  [local(): out_grad = lax.psum_scatter(grad_out, 'dp', scatter_dimension=0, tiled=True)]
    dot_general x24 -> x11, matrix products: 203 us -> 27 us  [the longest x1 3.62 us: local(): jnp.einsum('sih,sif->hf', act, latents_cot, preferred_element_type=F32)]
    all_gather x6 -> x1, waiting for transfers between devices: 159 us -> 0.02 us  [local(): lax.all_gather(jnp.concatenate([out_weight, mlp_in_weight, mlp_out_weight...]
    pallas_call x0 -> x6, Pallas kernels: none -> 105 us  [the longest x1 23.8 us: attend_back(): pl.pallas_call(functools.partial(attend_back_kernel, chunk, scale, 1.0 /...]
    unnamed x2 -> x0, blocking collectives: 76.2 us -> none
    ppermute x0 -> x48, waiting for transfers between devices: none -> 73.9 us  [the longest x36 49.6 us: scatter_sum(): total = total + lax.ppermute(sent, 'dp', self.shift(dim, r)).astype(F32)]
    ppermute x0 -> x48, starting transfers between devices: none -> 67 us  [the longest x36 51.1 us: scatter_sum(): total = total + lax.ppermute(sent, 'dp', self.shift(dim, r)).astype(F32)]
    all_gather x1 -> x0, blocking collectives: 46.1 us -> none  [local(): lax.all_gather(latent_array, 'dp', axis=0, tiled=True)]
  transfers between devices with their start and end apart: 13 -> 50, of which waited for: 10 -> 22; matrix products, arithmetic and copies ran while one was open for 17% -> 14% of each run, Pallas kernels for 0% -> 21%
where the time goes in v1:
time: 396 us; the launch traced here: 390 us
  Pallas kernels  105 us (27%)
  waiting for transfers between devices  74.3 us (19%)
  starting transfers between devices  67 us (17%)
  local copies, waits for them, and re-layouts  56.7 us (14%)
  other arithmetic  45 us (11%)
  matrix products  27 us (7%)
  between operations  15.3 us (4%)
    ppermute x36, starting transfers between devices, scatter_sum(): total = total + lax.ppermute(sent, 'dp', self.shift(dim, r)).astype(F32)  51.1 us
    ppermute x36, waiting for transfers between devices, scatter_sum(): total = total + lax.ppermute(sent, 'dp', self.shift(dim, r)).astype(F32)  49.6 us
    ppermute x12, waiting for transfers between devices, gather(): parts.append(lax.ppermute(stack, 'dp', self.shift(dim, k - r)))  24.3 us
    pallas_call x1, Pallas kernels, attend_back(): pl.pallas_call(functools.partial(attend_back_kernel, chunk, scale, 1.0 /...  23.8 us
    pallas_call x1, Pallas kernels, kv_grad(): pl.pallas_call(kv_grad_kernel, grid=(seqs, slots // tile), in_specs=[colu...  20.7 us
    pallas_call x1, Pallas kernels, project(): pl.pallas_call(project_kernel, grid=(seqs, slots // tile), in_specs=[rows...  18.7 us
    pallas_call x1, Pallas kernels, input_grad(): pl.pallas_call(input_grad_kernel, grid=(seqs, slots // tile), in_specs=[c...  18.6 us
    pallas_call x1, Pallas kernels, attend(): pl.pallas_call(functools.partial(attend_kernel, chunk, scale), grid=(seqs...  16.9 us
  transfers between devices with their start and end apart: 50, of which 22 were waited for; matrix products, arithmetic and copies ran while one was open for 14% of the time, Pallas kernels for 21%

profile of v1, /device:TPU:0, one launch (start us, length us, event | category | flops | bytes accessed | tf_op | source)
XLA Modules:
  0.0 390.3 jit_solution(10488936361059861601)
XLA Ops:
  39.0 6.5 %collective-permute-done.9 = bf16[4,56,768]{2,1,0:T(8,128)(2,1)S(1)} collective-permute-done((bf16[4,56,768]{2,1,0:T(8,128)(2,1)S(1)}, bf16[4,56,768]{2,1,0:T(8,128)(2,1)S(1)}, u32[]{:S(2)}, u32[]{:S(2)}) %collective-permute-start.9) | collective-permute-done | bytes 344096 | tf_op jit(solution)/shard_map/ppermute | solution.py:93
  47.7 10.3 %collective-permute-done.4 = bf16[8,48,768]{2,1,0:T(8,128)(2,1)S(1)} collective-permute-done((bf16[8,48,768]{2,1,0:T(8,128)(2,1)S(1)}, bf16[8,48,768]{2,1,0:T(8,128)(2,1)S(1)}, u32[]{:S(2)}, u32[]{:S(2)}) %collective-permute-start.4) | collective-permute-done | bytes 589856 | tf_op jit(solution)/shard_map/ppermute | solution.py:93
  58.9 4.8 %collective-permute-done.10 = bf16[8,56,768]{2,1,0:T(8,128)(2,1)S(1)} collective-permute-done((bf16[8,56,768]{2,1,0:T(8,128)(2,1)S(1)}, bf16[8,56,768]{2,1,0:T(8,128)(2,1)S(1)}, u32[]{:S(2)}, u32[]{:S(2)}) %collective-permute-start.10) | collective-permute-done | bytes 688160 | tf_op jit(solution)/shard_map/ppermute | solution.py:93
  72.0 6.2 %prepare.1 = (bf16[1536,768]{1,0:T(8,128)(2,1)}, bf16[1280,768]{1,0:T(8,128)(2,1)}, bf16[256,1280]{1,0:T(8,128)(2,1)}, bf16[8,256,112]{2,1,0:T(8,128)(2,1)}, bf1...) custom-call(s32[2,32]{1,0:T(2,128)} %pad_add_fusion.place_ref, ...), custom_call_target="tpu_custom_call" | custom-call | tf_op jit(solution)/shard_map/prepare/pallas_call | solution.py:178
  80.8 18.7 %project.1 = (bf16[2,2048,768]{2,1,0:T(8,128)(2,1)}, bf16[2,8,112,2048]{3,2,1,0:T(8,128)(2,1)}, bf16[2,8,112,2048]{3,2,1,0:T(8,128)(2,1)}) custom-call(bf16[2,2048,768]{2,1,0:T(8,128)(2,1)} %x_ref.3, f32[1,768]{1,0:T(1,128)} %get-tuple-element.32.gain_ref, bf16[1536,768]{1,0:T(8,128)(2,1)} %get-tuple-element.33.w_ref, f32[2,1,2048]{2,1,0:T(1,128)} %broadcast_in_dim.23.addend_ref), custom_call_target="tpu_custom_call" | custom-call | flops 9663676416 | bytes 31457280 | tf_op jit(solution)/shard_map/project/pallas_call | solution.py:210
  99.6 16.9 %attend.1 = (f32[2,256,768]{2,1,0:T(8,128)}, f32[2,8,256,128]{3,2,1,0:T(8,128)}) custom-call(bf16[8,256,112]{2,1,0:T(8,128)(2,1)} %get-tuple-element.31.q_ref, bf16[2,8,112,2048]{3,2,1,0:T(8,128)(2,1)} %get-tuple-element.34.k_ref, bf16[2,8,112,2048]{3,2,1,0:T(8,128)(2,1)} %get-tuple-element.35.v_ref), custom_call_target="tpu_custom_call" | custom-call | flops 12884901888 | bytes 14680064 | tf_op jit(solution)/shard_map/attend/pallas_call | solution.py:259
  122.4 3.5 fusion.80
  138.2 3.6 fusion
  150.4 7.3 %fusion.10 = bf16[2,256,1280]{2,1,0:T(8,128)(2,1)S(1)} fusion(f32[2,256,1280]{2,1,0:T(8,128)} %copy-done.16, u8[256,1280]{1,0:T(8,128)(4,1)} %get-tuple-element.51, u8[256,1280]{1,0:T(8,128)(4,1)S(1)} %get-tuple-element.50), kind=kLoop, calls=%fused_computation.25 | loop fusion | flops 45875200 | bytes 4587520 | tf_op jit(solution)/shard_map/convert_element_type | solution.py:468
  160.7 3.6 fusion.1
  168.9 4.1 %fusion.21 = (bf16[2,8,256,1]{3,2,1,0:T(8,128)(2,1)}, bf16[2,8,256,1]{3,2,1,0:T(8,128)(2,1)}) fusion(f32[2,8,256,1]{3,2,1,0:T(8,128)} %copy.64, f32[2,8,256,1]{3,2,1,0:T(8,128)} %copy.65), kind=kLoop, calls=%fused_computation.54 | loop fusion | flops 20480 | bytes 49152 | tf_op jit(solution)/shard_map/convert_element_type | solution.py:498
  174.2 6.8 %concatenate.73.dm_ref = bf16[2,8,256,112]{3,2,1,0:T(8,128)(2,1)} concatenate(bf16[2,8,256,96]{3,2,1,0:T(8,128)(2,1)S(1)} %bitcast.245, bf16[2,8,256,1]{3,2,1,0:T(8,128)(2,1)S(1)} %copy.66, bf16[2,8,256,1]{3,2,1,0:T(8,128)(2,1)} %get-tuple-element.67, bf16[2,8,256,1]{3,2,1,0:T(8,128)(2,1)} %get-tuple-element.66, bf16[2,8,256,13]{3,2,1,0:T(8,128)(2,1)} %broadcast_in_dim.44), dimensions={3} | concatenate | bytes 1835008 | tf_op jit(solution)/shard_map/concatenate | solution.py:500
  181.1 23.8 %attend_back.1 = (bf16[2,256,768]{2,1,0:T(8,128)(2,1)}, bf16[2,768,2048]{2,1,0:T(8,128)(2,1)}, bf16[2,768,2048]{2,1,0:T(8,128)(2,1)}) custom-call(bf16[8,256,112]{2,1,0:T(8,128)(2,1)} %get-tuple-element.31.q_ref, bf16[768,256]{1,0:T(8,128)(2,1)} %get-tuple-element.38.qt_ref, bf16[2,8,112,2048]{3,2,1,0:T(8,128)(2,1)} %get-tuple-element.34.k_ref, ...), custom_call_target="tpu_custom_call" | custom-call | flops 32212254720 | bytes 29360128 | tf_op jit(solution)/shard_map/attend_back/pallas_call | solution.py:310
  215.7 18.6 %input_grad.1 = bf16[2,2048,768]{2,1,0:T(8,128)(2,1)} custom-call(bf16[2,768,2048]{2,1,0:T(8,128)(2,1)} %get-tuple-element.40.dk_ref, bf16[2,768,2048]{2,1,0:T(8,128)(2,1)} %get-tuple-element.41.dv_ref, bf16[1536,768]{1,0:T(8,128)(2,1)} %get-tuple-element.33.w_ref, f32[1,768]{1,0:T(1,128)} %get-tuple-element.32.gain_ref, bf16[2,2048,768]{2,1,0:T(8,128)(2,1)} %x_ref.3), custom_call_target="tpu_custom_call" | custom-call | flops 9663676416 | bytes 25165824 | tf_op jit(solution)/shard_map/input_grad/pallas_call | solution.py:391
  234.2 20.7 %kv_grad.1 = (bf16[768,768]{1,0:T(8,128)(2,1)}, bf16[768,768]{1,0:T(8,128)(2,1)}) custom-call(bf16[2,768,2048]{2,1,0:T(8,128)(2,1)} %get-tuple-element.40.dk_ref, bf16[2,768,2048]{2,1,0:T(8,128)(2,1)} %get-tuple-element.41.dv_ref, bf16[2,2048,768]{2,1,0:T(8,128)(2,1)} %get-tuple-element.45.normed_ref), custom_call_target="tpu_custom_call" | custom-call | flops 9663676416 | bytes 18874368 | tf_op jit(solution)/shard_map/kv_grad/pallas_call | solution.py:363
  282.6 5.6 %collective-permute-done.19 = bf16[4,2,24,768]{3,2,1,0:T(8,128)(2,1)S(1)} collective-permute-done((bf16[4,2,24,768]{3,2,1,0:T(8,128)(2,1)S(1)}, bf16[4,2,24,768]{3,2,1,0:T(8,128)(2,1)S(1)}, u32[]{:S(2)}, u32[]{:S(2)}) %collective-permute-start.19) | collective-permute-done | bytes 294944 | tf_op jit(solution)/shard_map/ppermute | solution.py:122
  290.7 3.9 collective-permute-start.33
  322.6 4.8 %collective-permute-done.16 = bf16[32,768]{1,0:T(8,128)(2,1)S(1)} collective-permute-done((bf16[32,768]{1,0:T(8,128)(2,1)S(1)}, bf16[32,768]{1,0:T(8,128)(2,1)S(1)}, u32[]{:S(2)}, u32[]{:S(2)}) %collective-permute-start.16) | collective-permute-done | bytes 49184 | tf_op jit(solution)/shard_map/ppermute | solution.py:122
  334.2 13.3 %collective-permute-done.37 = bf16[4,2,40,1280]{3,2,0,1:T(8,128)(2,1)S(1)} collective-permute-done((bf16[4,2,40,1280]{3,2,0,1:T(8,128)(2,1)S(1)}, bf16[4,2,40,1280]{3,2,0,1:T(8,128)(2,1)S(1)}, u32[]{:S(2)}, u32[]{:S(2)}) %collective-permute-start.37) | collective-permute-done | bytes 819232 | tf_op jit(solution)/shard_map/ppermute | solution.py:122
  349.7 3.5 collective-permute-start.44
  353.2 4.8 %collective-permute-done.38 = bf16[4,40,1280]{2,1,0:T(8,128)(2,1)S(1)} collective-permute-done((bf16[4,40,1280]{2,1,0:T(8,128)(2,1)S(1)}, bf16[4,40,1280]{2,1,0:T(8,128)(2,1)S(1)}, u32[]{:S(2)}, u32[]{:S(2)}) %collective-permute-start.38) | collective-permute-done | bytes 409632 | tf_op jit(solution)/shard_map/ppermute | solution.py:122
  364.4 3.3 collective-permute-start.47
  367.6 4.6 %collective-permute-start.46 = (bf16[40,1280]{1,0:T(8,128)(2,1)S(1)}, bf16[40,1280]{1,0:T(8,128)(2,1)S(1)}, u32[]{:S(2)}, u32[]{:S(2)}) collective-permute-start(bf16[40,1280]{1,0:T(8,128)(2,1)S(1)} %get-tuple-element.82), channel_id=1, source_target_pairs={{0,16},{1,17},{2,18},{3,19},{4,20},{5,21},{6,22},{7,23},{8,24},{9,... | collective-permute-start | bytes 307208 | tf_op jit(solution)/shard_map/ppermute | solution.py:122
  372.3 5.5 %collective-permute-done.40 = bf16[40,1280]{1,0:T(8,128)(2,1)S(1)} collective-permute-done((bf16[40,1280]{1,0:T(8,128)(2,1)S(1)}, bf16[40,1280]{1,0:T(8,128)(2,1)S(1)}, u32[]{:S(2)}, u32[]{:S(2)}) %collective-permute-start.40) | collective-permute-done | bytes 102432 | tf_op jit(solution)/shard_map/ppermute | solution.py:122
  (305 shorter events, 170.2 us)
Async XLA Ops:
  7.2 113.5 %all-gather.3.cloned.1.call-start = ((), (), s32[]{:S(2)}) async-start(), calls=%async_computation.2 | async-start | bytes 8785920 | tf_op jit(solution)/shard_map/all_gather | solution.py:431
  8.9 374.1 %reduce-scatter.2.cloned.1.call-start = ((), (), s32[]{:S(2)}) async-start(), calls=%async_computation.1 | async-start | bytes 4055040 | tf_op jit(solution)/shard_map/reduce_scatter | solution.py:490
  10.5 14.5 %collective-permute-start.2 = (bf16[1,48,768]{2,1,0:T(8,128)(2,1)S(1)}, bf16[1,48,768]{2,1,0:T(8,128)(2,1)S(1)}, u32[]{:S(2)}, u32[]{:S(2)}) collective-permute-start(bf16[1,48,768]{2,1,0:T(8,128)(2,1)S(1)} %maximum_bitcast_fusion.1), channel_id=1, source_target_pairs={{0,8},{1,9},{2,10},{3,11},{4,12},{5,13},{6,14},{7,15},{8,16},{9,17... | collective-permute-start | bytes 221192 | tf_op jit(solution)/shard_map/ppermute | solution.py:93
  13.5 14.4 %collective-permute-start.1 = (bf16[1,48,768]{2,1,0:T(8,128)(2,1)S(1)}, bf16[1,48,768]{2,1,0:T(8,128)(2,1)S(1)}, u32[]{:S(2)}, u32[]{:S(2)}) collective-permute-start(bf16[1,48,768]{2,1,0:T(8,128)(2,1)S(1)} %maximum_bitcast_fusion.1), channel_id=1, source_target_pairs={{0,16},{1,17},{2,18},{3,19},{4,20},{5,21},{6,22},{7,23},{8,24},{9,... | collective-permute-start | bytes 221192 | tf_op jit(solution)/shard_map/ppermute | solution.py:93
  16.1 11.8 %collective-permute-start = (bf16[1,48,768]{2,1,0:T(8,128)(2,1)S(1)}, bf16[1,48,768]{2,1,0:T(8,128)(2,1)S(1)}, u32[]{:S(2)}, u32[]{:S(2)}) collective-permute-start(bf16[1,48,768]{2,1,0:T(8,128)(2,1)S(1)} %maximum_bitcast_fusion.1), channel_id=1, source_target_pairs={{0,24},{1,25},{2,26},{3,27},{4,28},{5,29},{6,30},{7,31},{8,0},{9,1... | collective-permute-start | bytes 221192 | tf_op jit(solution)/shard_map/ppermute | solution.py:93
  21.9 12.2 %collective-permute-start.7 = (bf16[1,56,768]{2,1,0:T(8,128)(2,1)S(1)}, bf16[1,56,768]{2,1,0:T(8,128)(2,1)S(1)}, u32[]{:S(2)}, u32[]{:S(2)}) collective-permute-start(bf16[1,56,768]{2,1,0:T(8,128)(2,1)S(1)} %maximum_bitcast_fusion), channel_id=1, source_target_pairs={{0,16},{1,17},{2,18},{3,19},{4,20},{5,21},{6,22},{7,23},{8,24},{9,... | collective-permute-start | bytes 258056 | tf_op jit(solution)/shard_map/ppermute | solution.py:93
  38.4 19.6 %collective-permute-start.4 = (bf16[8,48,768]{2,1,0:T(8,128)(2,1)S(1)}, bf16[8,48,768]{2,1,0:T(8,128)(2,1)S(1)}, u32[]{:S(2)}, u32[]{:S(2)}) collective-permute-start(bf16[8,48,768]{2,1,0:T(8,128)(2,1)S(1)} %get-tuple-element.91), channel_id=1, source_target_pairs={{0,4},{1,5},{2,6},{3,7},{4,0},{5,1},{6,2},{7,3},{8,12},{9,13},{10,... | collective-permute-start | bytes 1769480 | tf_op jit(solution)/shard_map/ppermute | solution.py:93
  46.3 17.5 %collective-permute-start.10 = (bf16[8,56,768]{2,1,0:T(8,128)(2,1)S(1)}, bf16[8,56,768]{2,1,0:T(8,128)(2,1)S(1)}, u32[]{:S(2)}, u32[]{:S(2)}) collective-permute-start(bf16[8,56,768]{2,1,0:T(8,128)(2,1)S(1)} %get-tuple-element.88), channel_id=1, source_target_pairs={{0,2},{1,3},{2,0},{3,1},{4,6},{5,7},{6,4},{7,5},{8,10},{9,11},{10,... | collective-permute-start | bytes 2064392 | tf_op jit(solution)/shard_map/ppermute | solution.py:93
  213.0 115.9 %collective-permute-start.36 = (bf16[4,2,2,40,1280]{4,3,0,2,1:T(8,128)(2,1)}, bf16[4,2,2,40,1280]{4,3,0,2,1:T(8,128)(2,1)}, u32[]{:S(2)}, u32[]{:S(2)}) collective-permute-start(bf16[4,2,2,40,1280]{4,3,0,2,1:T(8,128)(2,1)} %bitcast.242), channel_id=1, source_target_pairs={{0,1},{1,0},{2,3},{3,2},{4,5},{5,4},{6,7},{7,6},{8,9},{9,8},{10,11... | collective-permute-start | bytes 4915208 | tf_op jit(solution)/shard_map/ppermute | solution.py:122
  261.2 12.5 %collective-permute-start.18 = (bf16[4,2,2,24,768]{4,3,2,1,0:T(8,128)(2,1)}, bf16[4,2,2,24,768]{4,3,2,1,0:T(8,128)(2,1)}, u32[]{:S(2)}, u32[]{:S(2)}) collective-permute-start(bf16[4,2,2,24,768]{4,3,2,1,0:T(8,128)(2,1)} %dynamic-slice_bitcast_fusion.3), channel_id=1, source_target_pairs={{0,1},{1,0},{2,3},{3,2},{4,5},{5,4},{6,7},{7,6},{8,9},{9,8},{10,11... | collective-permute-start | bytes 1769480 | tf_op jit(solution)/shard_map/ppermute | solution.py:122
  263.9 11.5 %collective-permute-start.12 = (bf16[4,2,2,32,768]{4,3,2,1,0:T(8,128)(2,1)}, bf16[4,2,2,32,768]{4,3,2,1,0:T(8,128)(2,1)}, u32[]{:S(2)}, u32[]{:S(2)}) collective-permute-start(bf16[4,2,2,32,768]{4,3,2,1,0:T(8,128)(2,1)} %dynamic-slice_bitcast_fusion.2), channel_id=1, source_target_pairs={{0,1},{1,0},{2,3},{3,2},{4,5},{5,4},{6,7},{7,6},{8,9},{9,8},{10,11... | collective-permute-start | bytes 2359304 | tf_op jit(solution)/shard_map/ppermute | solution.py:122
  275.0 13.3 %collective-permute-start.19 = (bf16[4,2,24,768]{3,2,1,0:T(8,128)(2,1)S(1)}, bf16[4,2,24,768]{3,2,1,0:T(8,128)(2,1)S(1)}, u32[]{:S(2)}, u32[]{:S(2)}) collective-permute-start(bf16[4,2,24,768]{3,2,1,0:T(8,128)(2,1)S(1)} %dynamic-slice_bitcast_fusion.9), channel_id=1, source_target_pairs={{0,4},{1,5},{2,6},{3,7},{4,0},{5,1},{6,2},{7,3},{8,12},{9,13},{10,... | collective-permute-start | bytes 884744 | tf_op jit(solution)/shard_map/ppermute | solution.py:122
  276.9 33.2 %collective-permute-start.13 = (bf16[4,2,32,768]{3,2,1,0:T(8,128)(2,1)S(1)}, bf16[4,2,32,768]{3,2,1,0:T(8,128)(2,1)S(1)}, u32[]{:S(2)}, u32[]{:S(2)}) collective-permute-start(bf16[4,2,32,768]{3,2,1,0:T(8,128)(2,1)S(1)} %dynamic-slice_bitcast_fusion.6), channel_id=1, source_target_pairs={{0,2},{1,3},{2,0},{3,1},{4,6},{5,7},{6,4},{7,5},{8,10},{9,11},{10,... | collective-permute-start | bytes 1179656 | tf_op jit(solution)/shard_map/ppermute | solution.py:122
  278.3 12.3 %collective-permute-start.32 = (bf16[4,24,768]{2,1,0:T(8,128)(2,1)S(1)}, bf16[4,24,768]{2,1,0:T(8,128)(2,1)S(1)}, u32[]{:S(2)}, u32[]{:S(2)}) collective-permute-start(bf16[4,24,768]{2,1,0:T(8,128)(2,1)S(1)} %dynamic-slice_bitcast_fusion.11), channel_id=1, source_target_pairs={{0,4},{1,5},{2,6},{3,7},{4,0},{5,1},{6,2},{7,3},{8,12},{9,13},{10,... | collective-permute-start | bytes 442376 | tf_op jit(solution)/shard_map/ppermute | solution.py:122
  282.0 12.5 %collective-permute-start.26 = (bf16[4,24,768]{2,1,0:T(8,128)(2,1)S(1)}, bf16[4,24,768]{2,1,0:T(8,128)(2,1)S(1)}, u32[]{:S(2)}, u32[]{:S(2)}) collective-permute-start(bf16[4,24,768]{2,1,0:T(8,128)(2,1)S(1)} %dynamic-slice_bitcast_fusion.12), channel_id=1, source_target_pairs={{0,2},{1,3},{2,0},{3,1},{4,6},{5,7},{6,4},{7,5},{8,10},{9,11},{10,... | collective-permute-start | bytes 442376 | tf_op jit(solution)/shard_map/ppermute | solution.py:122
  304.0 28.7 %collective-permute-start.42 = (bf16[4,2,2,40,1280]{4,3,0,1,2:T(8,128)(2,1)S(1)}, bf16[4,2,2,40,1280]{4,3,0,1,2:T(8,128)(2,1)S(1)}, u32[]{:S(2)}, u32[]{:S(2)}) collective-permute-start(bf16[4,2,2,40,1280]{4,3,0,1,2:T(8,128)(2,1)S(1)} %bitcast.263), channel_id=1, source_target_pairs={{0,1},{1,0},{2,3},{3,2},{4,5},{5,4},{6,7},{7,6},{8,9},{9,8},{10,11... | collective-permute-start | bytes 4915208 | tf_op jit(solution)/shard_map/ppermute | solution.py:122
  330.8 16.8 %collective-permute-start.37 = (bf16[4,2,40,1280]{3,2,0,1:T(8,128)(2,1)S(1)}, bf16[4,2,40,1280]{3,2,0,1:T(8,128)(2,1)S(1)}, u32[]{:S(2)}, u32[]{:S(2)}) collective-permute-start(bf16[4,2,40,1280]{3,2,0,1:T(8,128)(2,1)S(1)} %dynamic-slice_bitcast_fusion.1), channel_id=1, source_target_pairs={{0,4},{1,5},{2,6},{3,7},{4,0},{5,1},{6,2},{7,3},{8,12},{9,13},{10,... | collective-permute-start | bytes 2457608 | tf_op jit(solution)/shard_map/ppermute | solution.py:122
  333.3 16.2 %collective-permute-start.43 = (bf16[4,2,40,1280]{3,2,0,1:T(8,128)(2,1)S(1)}, bf16[4,2,40,1280]{3,2,0,1:T(8,128)(2,1)S(1)}, u32[]{:S(2)}, u32[]{:S(2)}) collective-permute-start(bf16[4,2,40,1280]{3,2,0,1:T(8,128)(2,1)S(1)} %dynamic-slice_bitcast_fusion), channel_id=1, source_target_pairs={{0,2},{1,3},{2,0},{3,1},{4,6},{5,7},{6,4},{7,5},{8,10},{9,11},{10,... | collective-permute-start | bytes 2457608 | tf_op jit(solution)/shard_map/ppermute | solution.py:122
  349.7 13.8 %collective-permute-start.44 = (bf16[4,40,1280]{2,1,0:T(8,128)(2,1)S(1)}, bf16[4,40,1280]{2,1,0:T(8,128)(2,1)S(1)}, u32[]{:S(2)}, u32[]{:S(2)}) collective-permute-start(bf16[4,40,1280]{2,1,0:T(8,128)(2,1)S(1)} %dynamic-slice_bitcast_fusion.4), channel_id=1, source_target_pairs={{0,4},{1,5},{2,6},{3,7},{4,0},{5,1},{6,2},{7,3},{8,12},{9,13},{10,... | collective-permute-start | bytes 1228808 | tf_op jit(solution)/shard_map/ppermute | solution.py:122
  360.8 11.5 %collective-permute-start.41 = (bf16[40,1280]{1,0:T(8,128)(2,1)S(1)}, bf16[40,1280]{1,0:T(8,128)(2,1)S(1)}, u32[]{:S(2)}, u32[]{:S(2)}) collective-permute-start(bf16[40,1280]{1,0:T(8,128)(2,1)S(1)} %get-tuple-element.84), channel_id=1, source_target_pairs={{0,24},{1,25},{2,26},{3,27},{4,28},{5,29},{6,30},{7,31},{8,0},{9,1... | collective-permute-start | bytes 307208 | tf_op jit(solution)/shard_map/ppermute | solution.py:122
  362.1 15.7 %collective-permute-start.40 = (bf16[40,1280]{1,0:T(8,128)(2,1)S(1)}, bf16[40,1280]{1,0:T(8,128)(2,1)S(1)}, u32[]{:S(2)}, u32[]{:S(2)}) collective-permute-start(bf16[40,1280]{1,0:T(8,128)(2,1)S(1)} %get-tuple-element.85), channel_id=1, source_target_pairs={{0,16},{1,17},{2,18},{3,19},{4,20},{5,21},{6,22},{7,23},{8,24},{9,... | collective-permute-start | bytes 307208 | tf_op jit(solution)/shard_map/ppermute | solution.py:122
  363.7 15.4 %collective-permute-start.45 = (bf16[40,1280]{1,0:T(8,128)(2,1)S(1)}, bf16[40,1280]{1,0:T(8,128)(2,1)S(1)}, u32[]{:S(2)}, u32[]{:S(2)}) collective-permute-start(bf16[40,1280]{1,0:T(8,128)(2,1)S(1)} %get-tuple-element.80), channel_id=1, source_target_pairs={{0,8},{1,9},{2,10},{3,11},{4,12},{5,13},{6,14},{7,15},{8,16},{9,17... | collective-permute-start | bytes 307208 | tf_op jit(solution)/shard_map/ppermute | solution.py:122
  364.4 14.8 %collective-permute-start.47 = (bf16[40,1280]{1,0:T(8,128)(2,1)S(1)}, bf16[40,1280]{1,0:T(8,128)(2,1)S(1)}, u32[]{:S(2)}, u32[]{:S(2)}) collective-permute-start(bf16[40,1280]{1,0:T(8,128)(2,1)S(1)} %get-tuple-element.81), channel_id=1, source_target_pairs={{0,24},{1,25},{2,26},{3,27},{4,28},{5,29},{6,30},{7,31},{8,0},{9,1... | collective-permute-start | bytes 307208 | tf_op jit(solution)/shard_map/ppermute | solution.py:122
  367.6 14.3 %collective-permute-start.46 = (bf16[40,1280]{1,0:T(8,128)(2,1)S(1)}, bf16[40,1280]{1,0:T(8,128)(2,1)S(1)}, u32[]{:S(2)}, u32[]{:S(2)}) collective-permute-start(bf16[40,1280]{1,0:T(8,128)(2,1)S(1)} %get-tuple-element.82), channel_id=1, source_target_pairs={{0,16},{1,17},{2,18},{3,19},{4,20},{5,21},{6,22},{7,23},{8,24},{9,... | collective-permute-start | bytes 307208 | tf_op jit(solution)/shard_map/ppermute | solution.py:122
  (64 other events, 626.0 us)
Sparse Core Ops, SparseCore 0:
  10.8 90.1 all-gather.2
  267.4 115.5 reduce-scatter.1

commit v2 on v1

v2 whole, which is shorter than its diff:
```python
import functools
import math

import jax
import jax.numpy as jnp
from jax import lax
from jax.experimental import pallas as pl
from jax.experimental.pallas import tpu as pltpu
from jax.sharding import PartitionSpec as P

HEADS = 8
HEAD = 96
PADDED = 112
MASKED = -1e30
VMEM = 56 * 1024 * 1024
F32 = jnp.float32
BF16 = jnp.bfloat16


def nn(a, b):
    return lax.dot_general(a, b, (((1,), (0,)), ((), ())), preferred_element_type=F32)


def nt(a, b):
    return lax.dot_general(a, b, (((1,), (1,)), ((), ())), preferred_element_type=F32)


def tn(a, b):
    return lax.dot_general(a, b, (((0,), (0,)), ((), ())), preferred_element_type=F32)


def unit_rows(rows):
    centred = rows - jnp.mean(rows, axis=-1, keepdims=True)
    inverse = lax.rsqrt(jnp.mean(centred * centred, axis=-1, keepdims=True) + 1e-05)
    return centred * inverse, inverse


def norm_back(upstream, unit, inverse, gain):
    scaled = upstream * gain
    inner = (
        scaled
        - jnp.mean(scaled, axis=-1, keepdims=True)
        - unit * jnp.mean(scaled * unit, axis=-1, keepdims=True)
    )
    return inverse * inner


def grid_of(devices):
    known = {32: (4, 2, 2, 2), 128: (4, 4, 4, 2)}
    if devices in known:
        return known[devices]
    dims, left = [], devices
    while left > 1:
        step = next(f for f in (2, 3, 4, 5, 7, left) if left % f == 0)
        dims.insert(0, step)
        left //= step
    return tuple(dims)


class Grid:
    def __init__(self, devices):
        self.devices = devices
        self.dims = grid_of(devices)
        self.strides = tuple(math.prod(self.dims[i + 1 :]) for i in range(len(self.dims)))
        me = lax.axis_index("dp")
        self.mine = tuple((me // s) % k for s, k in zip(self.strides, self.dims))
        last = len(self.dims) - 1
        near = list(range(1, last))
        self.order_a = (0, *near[::-1], last) if last else (0,)
        self.order_b = (0, *near, last) if last else (0,)

    def shift(self, dim, r):
        k, s = self.dims[dim], self.strides[dim]
        pairs = []
        for i in range(self.devices):
            at = (i // s) % k
            pairs.append((i, i + (((at + r) % k) - at) * s))
        return pairs

    def found(self, order):
        sizes = [self.dims[dim] for dim in order]
        index = jnp.zeros((1,) * len(self.dims), jnp.int32)
        for n, dim in enumerate(order):
            step = math.prod(sizes[:n])
            away = (jnp.arange(self.dims[dim], dtype=jnp.int32) - self.mine[dim]) % self.dims[dim]
            shape = [1] * len(self.dims)
            shape[dim] = self.dims[dim]
            index = index + (away * step).reshape(shape)
        return index.reshape(-1)


class Pair:
    def __init__(self, grid, value, cut, forward):
        self.grid, self.cut = grid, cut
        self.left = list(zip(grid.order_a, grid.order_b))
        if not forward:
            self.left.reverse()
        self.parts = [value]

    def arrange(self):
        one, other = self.left[0]
        axis = self.parts[0].ndim - 2
        if one == other:
            if len(self.parts) == 2:
                self.parts = [jnp.concatenate(self.parts, axis=axis)]
            return [one]
        if len(self.parts) == 1:
            self.parts = jnp.split(self.parts[0], [self.cut], axis=axis)
        return [one, other]


class Gather(Pair):
    def __init__(self, grid, block, cut):
        super().__init__(grid, block[None], cut, True)

    def sends(self):
        self.dims = self.arrange()
        return [[part] for part in self.parts]

    def exchange(self, sent):
        grid = self.grid
        return [
            part + [lax.ppermute(part[0], "dp", grid.shift(dim, -r)) for r in range(1, grid.dims[dim])]
            for dim, part in zip(self.dims, sent)
        ]

    def receive(self, got):
        self.left.pop(0)
        self.parts = [jnp.concatenate(part, axis=0) for part in got]


class Scatter(Pair):
    def __init__(self, grid, whole, cut):
        super().__init__(grid, whole.reshape(*grid.dims, *whole.shape[1:]), cut, False)
        self.wire = whole.dtype
        self.rest = [list(range(len(grid.dims)))] * 2

    def sends(self):
        self.dims = self.arrange()
        sent = []
        for part, dim, rest in zip(self.parts, self.dims, self.rest):
            axis, k, me = rest.index(dim), self.grid.dims[dim], self.grid.mine[dim]
            sent.append(
                [lax.dynamic_index_in_dim(part, (me + r) % k, axis, keepdims=False) for r in range(k)]
            )
        return sent

    def exchange(self, sent):
        return [
            part[:1]
            + [lax.ppermute(piece, "dp", self.grid.shift(dim, r)) for r, piece in enumerate(part) if r]
            for dim, part in zip(self.dims, sent)
        ]

    def receive(self, got):
        self.rest = [[d for d in rest if d != dim] for rest, dim in zip(self.rest, self.left.pop(0))]
        totals = [sum(piece.astype(F32) for piece in part) for part in got]
        self.parts = [total.astype(self.wire) if self.left else total for total in totals]


def overlap(jobs, work=None, *args):
    live = [job for job in jobs if job.left]
    sent, args = lax.optimization_barrier(([job.sends() for job in live], args))
    got = [job.exchange(parts) for job, parts in zip(live, sent)]
    out = work(*args) if work else ()
    got, out = lax.optimization_barrier((got, out))
    for job, parts in zip(live, got):
        job.receive(parts)
    return out


def finish(jobs):
    while any(job.left for job in jobs):
        overlap(jobs)


def prepare_kv_kernel(cuts, place_ref, stack_ref, wt_ref, gin_ref, glat_ref, gmlp_ref, kv_ref):
    devices, _, width = stack_ref.shape
    k_rows = width // devices
    lines = []
    for d in range(devices):
        mine = slice(d * k_rows, (d + 1) * k_rows)
        values = stack_ref.at[place_ref[1, d]]
        kv_ref[mine, :width] = stack_ref[place_ref[0, d], :k_rows]
        kv_ref[mine, width:] = values[k_rows : 2 * k_rows]
        lines.append(values[2 * k_rows :][:1].astype(F32))
    first = 0
    for ref, size in zip((gin_ref, glat_ref, gmlp_ref), cuts):
        ref[...] = jnp.concatenate([line[:, first : first + size] for line in lines], axis=1)
        first += size
    for c in range(0, wt_ref.shape[0], width):
        wt_ref[c : c + width] = kv_ref[:, c : c + width].T


def prepare_kv(stack, places, cuts):
    devices, _, width = stack.shape
    vmem = pl.BlockSpec(memory_space=pltpu.VMEM)
    shapes = [((2 * width, width), BF16)] + [((1, devices * size), F32) for size in cuts]
    return pl.pallas_call(
        functools.partial(prepare_kv_kernel, cuts),
        in_specs=[pl.BlockSpec(memory_space=pltpu.SMEM), vmem],
        out_specs=[vmem] * len(shapes),
        out_shape=[jax.ShapeDtypeStruct(*s) for s in shapes],
        scratch_shapes=[pltpu.VMEM((width, 2 * width), BF16)],
        compiler_params=pltpu.CompilerParams(vmem_limit_bytes=VMEM),
        cost_estimate=pl.CostEstimate(flops=0, bytes_accessed=12_000_000, transcendentals=0),
        name="prepare_kv",
    )(places, stack)


def pack_rest(query, out, latents, q_top, join):
    width = query.shape[-1]
    k_rows, l_rows, l_width = out.shape[-2], latents.shape[-2], latents.shape[-1]
    spare = 2 * width - l_width
    ends = []
    for n in range(-(-(l_width - width) // spare)):
        piece = latents[..., width + n * spare : min(width + (n + 1) * spare, l_width)]
        short = spare - piece.shape[-1]
        ends.append(join([piece, jnp.zeros((*piece.shape[:-1], short), piece.dtype)], -1) if short else piece)
    short = k_rows - len(ends) * l_rows
    if short:
        ends.append(jnp.zeros((*out.shape[:-2], short, spare), out.dtype))
    beside = join([out[..., width:], join(ends, -2)], -1)
    return join([query[..., :q_top, :], out[..., :width], beside, query[..., q_top:, :], latents[..., :width]], -2)


def unpack_rest(rows, cuts):
    q_top, q_low, k_rows, l_rows, width, l_width = cuts
    spare = 2 * width - l_width
    second = q_top + k_rows
    third = second + k_rows
    found = [
        ("query", (0, q_top), (0, width), (0, q_top), (0, width)),
        ("out", (0, k_rows), (0, width), (q_top, second), (0, width)),
        ("out", (0, k_rows), (width, l_width), (second, third), (0, l_width - width)),
        ("query", (q_top, q_top + q_low), (0, width), (third, third + q_low), (0, width)),
        ("latents", (0, l_rows), (0, width), (third + q_low, third + q_low + l_rows), (0, width)),
    ]
    for n, at in enumerate(range(width, l_width, spare)):
        end = min(at + spare, l_width)
        start = second + n * l_rows
        found.append(
            ("latents", (0, l_rows), (at, end), (start, start + l_rows), (l_width - width, l_width - width + end - at))
        )
    return found


def prepare_q_kernel(cuts, place_ref, stack_ref, glat_ref, wq_ref, wo_ref, lat_ref, q_ref, qt_ref):
    devices = stack_ref.shape[0]
    q_top, _, k_rows = cuts[:3]
    wholes = {"query": wq_ref, "out": wo_ref, "latents": lat_ref}
    for d in range(devices):
        for what, rows, columns, at, beside in unpack_rest(stack_ref.shape[1], cuts):
            ref = wholes[what]
            base = d * (ref.shape[0] // devices)
            part = 0 if at[0] < q_top + k_rows else 1
            ref[base + rows[0] : base + rows[1], columns[0] : columns[1]] = stack_ref[
                place_ref[part, d], at[0] : at[1], beside[0] : beside[1]
            ]
    unit, _ = unit_rows(lat_ref[...].astype(F32))
    query = nn((unit * glat_ref[...]).astype(BF16), wq_ref[...])
    qt_ref[...] = query.T.astype(BF16)
    query = query.astype(BF16)
    column = lax.broadcasted_iota(jnp.int32, (query.shape[0], PADDED - HEAD), 1)
    ones = jnp.where(column == 0, 1.0, 0.0).astype(BF16)
    for h in range(HEADS):
        q_ref[h] = jnp.concatenate([query[:, h * HEAD : (h + 1) * HEAD], ones], axis=1)


def prepare_q(stack, gain, places, cuts):
    devices = stack.shape[0]
    q_top, q_low, k_rows, l_rows, width, l_width = cuts
    rows = devices * l_rows
    vmem = pl.BlockSpec(memory_space=pltpu.VMEM)
    shapes = [
        (devices * (q_top + q_low), width),
        (devices * k_rows, l_width),
        (rows, l_width),
        (HEADS, rows, PADDED),
        (width, rows),
    ]
    return pl.pallas_call(
        functools.partial(prepare_q_kernel, cuts),
        in_specs=[pl.BlockSpec(memory_space=pltpu.SMEM), vmem, vmem],
        out_specs=[vmem] * len(shapes),
        out_shape=[jax.ShapeDtypeStruct(s, BF16) for s in shapes],
        compiler_params=pltpu.CompilerParams(vmem_limit_bytes=VMEM),
        cost_estimate=pl.CostEstimate(flops=0, bytes_accessed=12_000_000, transcendentals=0),
        name="prepare_q",
    )(places, stack, gain)


def project_kernel(x_ref, gain_ref, w_ref, addend_ref, normed_ref, k_ref, v_ref):
    unit, _ = unit_rows(x_ref[0].astype(F32))
    normed = (unit * gain_ref[...]).astype(BF16)
    normed_ref[0] = normed
    slots = normed.shape[0]
    both = nt(w_ref[...], normed).astype(BF16)
    row = lax.broadcasted_iota(jnp.int32, (PADDED - HEAD, slots), 0)
    mask_rows = jnp.where(row == 0, jnp.broadcast_to(addend_ref[0], row.shape), 0.0).astype(BF16)
    one_rows = jnp.where(row < 3, 1.0, 0.0).astype(BF16)
    for h in range(HEADS):
        k_ref[0, h, :HEAD] = both[h * HEAD : (h + 1) * HEAD]
        k_ref[0, h, HEAD:] = mask_rows
        v_ref[0, h, :HEAD] = both[(HEADS + h) * HEAD : (HEADS + h + 1) * HEAD]
        v_ref[0, h, HEAD:] = one_rows


def project(seq, x, gain, weights, addend, tile=512):
    _, slots, width = x.shape
    rows = pl.BlockSpec((1, tile, width), lambda j: (0, j, 0))
    heads = pl.BlockSpec((1, HEADS, PADDED, tile), lambda j: (0, 0, 0, j))
    whole = lambda a: pl.BlockSpec(a.shape, lambda j: (0,) * a.ndim)
    return pl.pallas_call(
        project_kernel,
        grid=(slots // tile,),
        in_specs=[
            pl.BlockSpec((1, tile, width), lambda j: (seq, j, 0)),
            whole(gain),
            whole(weights),
            pl.BlockSpec((1, 1, tile), lambda j: (seq, 0, j)),
        ],
        out_specs=[rows, heads, heads],
        out_shape=[
            jax.ShapeDtypeStruct((1, slots, width), BF16),
            jax.ShapeDtypeStruct((1, HEADS, PADDED, slots), BF16),
            jax.ShapeDtypeStruct((1, HEADS, PADDED, slots), BF16),
        ],
        compiler_params=pltpu.CompilerParams(vmem_limit_bytes=VMEM),
        cost_estimate=pl.CostEstimate(
            flops=8 * slots * width * width, bytes_accessed=10 * slots * width, transcendentals=0
        ),
        name="project",
    )(x, gain, weights, addend)


def attend_kernel(chunk, scale, q_ref, k_ref, v_ref, mixed_ref, log_ref, score_ref):
    slots = k_ref.shape[-1]
    outs, logs = [], []
    for h in range(q_ref.shape[0]):
        score = score_ref.at[h % 2]
        top = None
        for j in range(0, slots, chunk):
            piece = nn(q_ref[h], k_ref[0, h, :, j : j + chunk])
            score[:, j : j + chunk] = piece
            for t in range(0, chunk, 128):
                part = piece[:, t : t + 128]
                top = part if top is None else jnp.maximum(top, part)
        top = jnp.max(top, axis=-1, keepdims=True)
        total = None
        for j in range(0, slots, chunk):
            power = jnp.exp2((score[:, j : j + chunk] - top) * scale).astype(BF16)
            piece = nt(power, v_ref[0, h, :, j : j + chunk])
            total = piece if total is None else total + piece
        weight = total[:, HEAD : HEAD + 1]
        outs.append(total[:, :HEAD] / weight)
        logs.append(top * scale + jnp.log2(weight))
    mixed_ref[0] = jnp.concatenate(outs, axis=1)
    for h, log in enumerate(logs):
        log_ref[0, h] = jnp.broadcast_to(log, log_ref.shape[2:])


def attend(q, k, v, chunk=1024, group=4):
    slots, rows = k.shape[-1], q.shape[1]
    scale = math.log2(math.e) / math.sqrt(HEAD)
    heads = pl.BlockSpec((1, group, PADDED, slots), lambda g: (0, g, 0, 0))
    return pl.pallas_call(
        functools.partial(attend_kernel, chunk, scale),
        grid=(HEADS // group,),
        in_specs=[pl.BlockSpec((group, rows, PADDED), lambda g: (g, 0, 0)), heads, heads],
        out_specs=[
            pl.BlockSpec((1, rows, group * HEAD), lambda g: (0, 0, g)),
            pl.BlockSpec((1, group, rows, 128), lambda g: (0, g, 0, 0)),
        ],
        out_shape=[
            jax.ShapeDtypeStruct((1, rows, HEADS * HEAD), F32),
            jax.ShapeDtypeStruct((1, HEADS, rows, 128), F32),
        ],
        scratch_shapes=[pltpu.VMEM((2, rows, slots), F32)],
        compiler_params=pltpu.CompilerParams(vmem_limit_bytes=VMEM),
        cost_estimate=pl.CostEstimate(
            flops=16 * rows * slots * HEADS * HEAD,
            bytes_accessed=4 * HEADS * PADDED * slots,
            transcendentals=HEADS * rows * slots,
        ),
        name="attend",
    )(q, k, v)


def attend_back_kernel(
    chunk, scale, factor, q_ref, qt_ref, k_ref, v_ref, log_ref, dm_ref, dmt_ref, dq_ref, dk_ref, dv_ref
):
    slots = k_ref.shape[-1]
    grads = []
    for h in range(q_ref.shape[0]):
        log = log_ref[0, h][:, :1]
        mine = slice(h * HEAD, (h + 1) * HEAD)
        total = None
        for j in range(0, slots, chunk):
            keys = k_ref[0, h, :, j : j + chunk]
            probs = jnp.exp2(nn(q_ref[h], keys) * scale - log)
            less = nn(dm_ref[0, h], v_ref[0, h, :, j : j + chunk])
            d_scores = (probs * less).astype(BF16)
            dv_ref[0, mine, j : j + chunk] = nn(dmt_ref[0, mine], probs.astype(BF16)).astype(BF16)
            dk_ref[0, mine, j : j + chunk] = (nn(qt_ref[mine], d_scores) * factor).astype(BF16)
            piece = nt(d_scores, keys[:HEAD])
            total = piece if total is None else total + piece
        grads.append((total * factor).astype(BF16))
    dq_ref[0] = jnp.concatenate(grads, axis=1)


def attend_back(seq, q, qt, k, v, log, dm, dmt, chunk=2048, group=4):
    slots = k.shape[-1]
    rows = q.shape[1]
    scale = math.log2(math.e) / math.sqrt(HEAD)
    heads = pl.BlockSpec((1, group, PADDED, slots), lambda g: (0, g, 0, 0))
    features = pl.BlockSpec((1, group * HEAD, slots), lambda g: (0, g, 0))
    return pl.pallas_call(
        functools.partial(attend_back_kernel, chunk, scale, 1.0 / math.sqrt(HEAD)),
        grid=(HEADS // group,),
        in_specs=[
            pl.BlockSpec((group, rows, PADDED), lambda g: (g, 0, 0)),
            pl.BlockSpec((group * HEAD, rows), lambda g: (g, 0)),
            heads,
            heads,
            pl.BlockSpec((1, group, rows, 128), lambda g: (0, g, 0, 0)),
            pl.BlockSpec((1, group, rows, PADDED), lambda g: (seq, g, 0, 0)),
            pl.BlockSpec((1, group * HEAD, rows), lambda g: (seq, g, 0)),
        ],
        out_specs=[pl.BlockSpec((1, rows, group * HEAD), lambda g: (0, 0, g)), features, features],
        out_shape=[
            jax.ShapeDtypeStruct((1, rows, HEADS * HEAD), BF16),
            jax.ShapeDtypeStruct((1, HEADS * HEAD, slots), BF16),
            jax.ShapeDtypeStruct((1, HEADS * HEAD, slots), BF16),
        ],
        compiler_params=pltpu.CompilerParams(vmem_limit_bytes=VMEM),
        cost_estimate=pl.CostEstimate(
            flops=40 * rows * slots * HEADS * HEAD,
            bytes_accessed=8 * HEADS * PADDED * slots,
            transcendentals=HEADS * rows * slots,
        ),
        name="attend_back",
    )(q, qt, k, v, log, dm, dmt)


def kv_grad_kernel(seqs, *refs):
    grads, normed, (out_ref, total_ref) = refs[: 2 * seqs], refs[2 * seqs : 3 * seqs], refs[3 * seqs :]
    devices = out_ref.shape[0]
    for n in range(2):
        piece = sum(nn(grads[2 * s + n][0], normed[s][0]) for s in range(seqs))

        @pl.when(pl.program_id(0) == 0)
        def _():
            total_ref[n] = piece

        @pl.when(pl.program_id(0) > 0)
        def _():
            total_ref[n] += piece

    @pl.when(pl.program_id(0) == pl.num_programs(0) - 1)
    def _():
        for n in range(2):
            whole = total_ref[n].T
            rows = whole.shape[0] // devices
            for d in range(devices):
                out_ref[d, n * rows : (n + 1) * rows] = whole[d * rows : (d + 1) * rows].astype(BF16)


def kv_grad(grads, normed, devices, tile=1024):
    seqs = len(normed)
    _, slots, width = normed[0].shape
    features = grads[0].shape[1]
    columns = pl.BlockSpec((1, features, tile), lambda j: (0, 0, j))
    shape = (devices, 2 * (width // devices), features)
    return pl.pallas_call(
        functools.partial(kv_grad_kernel, seqs),
        grid=(slots // tile,),
        in_specs=[columns] * (2 * seqs) + [pl.BlockSpec((1, tile, width), lambda j: (0, j, 0))] * seqs,
        out_specs=pl.BlockSpec(shape, lambda j: (0, 0, 0)),
        out_shape=jax.ShapeDtypeStruct(shape, BF16),
        scratch_shapes=[pltpu.VMEM((2, features, width), F32)],
        compiler_params=pltpu.CompilerParams(vmem_limit_bytes=VMEM),
        cost_estimate=pl.CostEstimate(
            flops=8 * seqs * slots * width * features, bytes_accessed=6 * seqs * slots * width, transcendentals=0
        ),
        name="kv_grad",
    )(*grads, *normed)


def query_grad_kernel(seqs, cuts, *refs):
    grads, (base_ref, gain_ref, wq_ref, rest_ref, go_ref, out_ref) = refs[:seqs], refs[seqs:]
    devices = out_ref.shape[0]
    unit, inverse = unit_rows(base_ref[...].astype(F32))
    normed = (unit * gain_ref[...]).astype(BF16)
    query = sum(tn(normed, grad[0]) for grad in grads)
    back = sum(nt(grad[0], wq_ref[...]) for grad in grads)
    latents = norm_back(back, unit, inverse, gain_ref[...]) + rest_ref[...]
    wholes = {"query": query, "out": go_ref[...].astype(F32), "latents": latents}
    for d in range(devices):
        pieces = []
        for what, rows, columns, at, beside in unpack_rest(out_ref.shape[1], cuts):
            whole = wholes[what]
            base = d * (whole.shape[0] // devices)
            out_ref[d, at[0] : at[1], beside[0] : beside[1]] = whole[
                base + rows[0] : base + rows[1], columns[0] : columns[1]
            ].astype(BF16)


def query_grad(grads, base, gain, w_query, rest, grad_out, devices, cuts):
    q_top, q_low, k_rows, l_rows, width, l_width = cuts
    vmem = pl.BlockSpec(memory_space=pltpu.VMEM)
    shape = (devices, q_top + q_low + 2 * k_rows + l_rows, width)
    return pl.pallas_call(
        functools.partial(query_grad_kernel, len(grads), cuts),
        in_specs=[vmem] * (len(grads) + 5),
        out_specs=vmem,
        out_shape=jax.ShapeDtypeStruct(shape, BF16),
        compiler_params=pltpu.CompilerParams(vmem_limit_bytes=VMEM),
        cost_estimate=pl.CostEstimate(
            flops=4 * len(grads) * base.shape[0] * l_width * width, bytes_accessed=12_000_000, transcendentals=0
        ),
        name="query_grad",
    )(*grads, base, gain, w_query, rest, grad_out)


def input_grad_kernel(dk_ref, dv_ref, w_ref, gain_ref, x_ref, *refs):
    out_ref = refs[-1]
    features = dk_ref.shape[1]
    upstream = tn(dk_ref[0], w_ref[:features]) + tn(dv_ref[0], w_ref[features:])
    unit, inverse = unit_rows(x_ref[0].astype(F32))
    out_ref[0] = norm_back(upstream, unit, inverse, gain_ref[...]).astype(BF16)


def input_grad(seq, first, steps, dk, dv, weights, gain, x, into=None, tile=512):
    features = dk.shape[1]
    width = x.shape[-1]
    columns = pl.BlockSpec((1, features, tile), lambda j: (0, 0, first + j))
    rows = pl.BlockSpec((1, tile, width), lambda j: (seq, first + j, 0))
    whole = lambda a: pl.BlockSpec(a.shape, lambda j: (0,) * a.ndim)
    args = [dk, dv, weights, gain, x] + ([] if into is None else [into])
    specs = [columns, columns, whole(weights), whole(gain), rows]
    return pl.pallas_call(
        input_grad_kernel,
        grid=(steps,),
        in_specs=specs + [pl.BlockSpec(memory_space=pl.ANY)] * (len(args) - len(specs)),
        out_specs=rows,
        out_shape=jax.ShapeDtypeStruct(x.shape, BF16),
        input_output_aliases={} if into is None else {5: 0},
        compiler_params=pltpu.CompilerParams(vmem_limit_bytes=VMEM),
        cost_estimate=pl.CostEstimate(
            flops=8 * steps * tile * width * features, bytes_accessed=8 * steps * tile * width, transcendentals=0
        ),
        name="input_grad",
    )(*args)


def gelu_parts(pre):
    cdf = 0.5 * (1.0 + lax.erf(pre * (1.0 / math.sqrt(2.0))))
    slope = cdf + pre * jnp.exp(-0.5 * pre * pre) * (1.0 / math.sqrt(2.0 * math.pi))
    return pre * cdf, slope


def feed_forward_kernel(seqs, *refs):
    mixed = refs[:seqs]
    base_ref, w_out_ref, w_mlp_ref, gain_ref, cot_ref = refs[seqs : seqs + 5]
    latents_ref, g_mlp_ref, g_out_ref, rest_ref, dm_ref, dmt_ref = refs[seqs + 5 : seqs + 11]
    mlp_ref, act_ref, pre_ref, attn_ref, mix_ref = refs[seqs + 11 :]
    _, rows, width = mixed[0].shape
    l_width = base_ref.shape[1]
    w_in_ref, w_back_ref = w_mlp_ref.at[:, :l_width], w_mlp_ref.at[:, l_width:]
    gain = gain_ref[...]
    base = base_ref[...].astype(F32)
    norms, ones, bars = [], [], []
    for s in range(seqs):
        mine = slice(s * rows, (s + 1) * rows)
        mix_ref[mine] = mixed[s][0].astype(BF16)
        x_one = base + nn(mix_ref[mine], w_out_ref[...])
        unit, inverse = unit_rows(x_one)
        mlp_ref[mine] = (unit * gain).astype(BF16)
        norms.append((unit, inverse))
        ones.append(x_one)
    for s in range(seqs):
        mine = slice(s * rows, (s + 1) * rows)
        pre = nn(mlp_ref[mine], w_in_ref[...])
        value, slope = gelu_parts(pre)
        act_ref[mine] = value.astype(BF16)
        pre_ref[mine] = (nt(cot_ref[s], w_back_ref[...]) * slope).astype(BF16)
    for s in range(seqs):
        mine = slice(s * rows, (s + 1) * rows)
        latents_ref[s] = (ones[s] + nn(act_ref[mine], w_back_ref[...])).astype(BF16)
        back = nt(pre_ref[mine], w_in_ref[...])
        bar = cot_ref[s].astype(F32) + norm_back(back, *norms[s], gain)
        attn_ref[mine] = bar.astype(BF16)
        bars.append(bar)
    rest_ref[...] = sum(bars)
    column = lax.broadcasted_iota(jnp.int32, (rows, PADDED - HEAD), 1)
    for s in range(seqs):
        mine = slice(s * rows, (s + 1) * rows)
        d_mixed = nt(attn_ref[mine], w_out_ref[...])
        dmt_ref[s] = d_mixed.T.astype(BF16)
        d_mixed = d_mixed.astype(BF16)
        for h in range(HEADS):
            part = d_mixed[:, h * HEAD : (h + 1) * HEAD]
            centre = -jnp.sum(part.astype(F32) * mixed[s][0, :, h * HEAD : (h + 1) * HEAD], axis=-1, keepdims=True)
            high = centre.astype(BF16).astype(F32)
            middle = (centre - high).astype(BF16).astype(F32)
            low = centre - high - middle
            pieces = jnp.where(column == 0, high, jnp.where(column == 1, middle, jnp.where(column == 2, low, 0.0)))
            dm_ref[s, h] = jnp.concatenate([part, pieces.astype(BF16)], axis=1)
    cot = jnp.concatenate([cot_ref[s] for s in range(seqs)], axis=0)
    devices = g_mlp_ref.shape[0]
    for n, whole in enumerate((tn(mlp_ref[...], pre_ref[...]), tn(act_ref[...], cot))):
        size = l_width // devices
        for d in range(devices):
            g_mlp_ref[d, n * size : (n + 1) * size] = whole[d * size : (d + 1) * size].astype(BF16)
    g_out_ref[...] = tn(mix_ref[...], attn_ref[...]).astype(BF16)


def feed_forward(mixed, base, w_out, w_mlp, gain, cot, devices):
    seqs = len(mixed)
    _, rows, width = mixed[0].shape
    l_width = base.shape[1]
    vmem = pl.BlockSpec(memory_space=pltpu.VMEM)
    shapes = [
        (cot.shape, BF16),
        ((devices, 2 * (l_width // devices), l_width), BF16),
        (w_out.shape, BF16),
        (base.shape, F32),
        ((seqs, HEADS, rows, PADDED), BF16),
        ((seqs, width, rows), BF16),
    ]
    many = seqs * rows
    return pl.pallas_call(
        functools.partial(feed_forward_kernel, seqs),
        in_specs=[vmem] * (seqs + 5),
        out_specs=[vmem] * len(shapes),
        out_shape=[jax.ShapeDtypeStruct(*s) for s in shapes],
        scratch_shapes=[pltpu.VMEM((many, l_width), BF16)] * 4 + [pltpu.VMEM((many, width), BF16)],
        compiler_params=pltpu.CompilerParams(vmem_limit_bytes=VMEM),
        cost_estimate=pl.CostEstimate(
            flops=6 * many * l_width * (width + 2 * l_width), bytes_accessed=24_000_000, transcendentals=0
        ),
        name="feed_forward",
    )(*mixed, base, w_out, w_mlp, gain, cot)


def local(
    byte_inputs,
    lengths,
    key_mask,
    latents_cot,
    latent_array,
    lat_gain,
    query_weight,
    in_gain,
    key_weight,
    value_weight,
    out_weight,
    mlp_gain,
    mlp_in_weight,
    mlp_out_weight,
):
    devices = lax.axis_size("dp")
    grid = Grid(devices)
    seqs, length, width = byte_inputs.shape
    k_rows, q_rows, l_rows = key_weight.shape[0], query_weight.shape[0], latent_array.shape[0]
    l_width = latent_array.shape[1]
    q_top = k_rows if q_rows > k_rows else q_rows // 2
    q_low = q_rows - q_top

    w_mlp = lax.all_gather(jnp.concatenate([mlp_in_weight, mlp_out_weight], axis=1), "dp", axis=0, tiled=True)

    gains = jnp.concatenate([in_gain, lat_gain, mlp_gain])
    sizes = (in_gain.shape[0], lat_gain.shape[0], mlp_gain.shape[0])
    gain_rows = jnp.broadcast_to(jnp.pad(gains, (0, width - gains.shape[0])), (8, width))
    first = Gather(grid, jnp.concatenate([key_weight, value_weight, gain_rows], axis=0), k_rows)
    packed = pack_rest(query_weight, out_weight, latent_array, q_top, jnp.concatenate)
    second = Gather(grid, packed, q_top + k_rows)
    cuts = (q_top, q_low, k_rows, l_rows, width, l_width)
    overlap([first])
    overlap([first, second])
    overlap([first])
    while first.left:
        overlap([first, second])
    positions = jnp.arange(length, dtype=jnp.int32)
    valid = (positions[None, :] < lengths[:, None]) & (key_mask == 1)
    addend = jnp.where(valid, 0.0, MASKED).astype(F32)[:, None]
    places = jnp.stack([grid.found(grid.order_a), grid.found(grid.order_b)])

    def begin(stack):
        ready = prepare_kv(stack, places, sizes)
        return ready, project(0, byte_inputs, ready[1], ready[0], addend)

    (kv_weights, g_in, g_lat, g_mlp), side = overlap([second], begin, first.parts[0])
    sides = [side]
    for s in range(1, seqs):
        sides.append(overlap([second], functools.partial(project, s), byte_inputs, g_in, kv_weights, addend))
    finish([second])
    w_query, w_out, base, q, qt = prepare_q(second.parts[0], g_lat, places, cuts)
    heard = [attend(q, k, v) for _, k, v in sides]
    latents, grad_mlp, grad_out, rest, dm, dmt = feed_forward(
        [mixed for mixed, _ in heard], base, w_out, w_mlp, g_mlp, latents_cot, devices
    )

    mlp_out = Scatter(grid, grad_mlp, q_rows)
    jobs = [mlp_out]
    backs = []
    for s, ((_, k, v), (_, log)) in enumerate(zip(sides, heard)):
        backs.append(overlap(jobs, functools.partial(attend_back, s), q, qt, k, v, log, dm, dmt))
    work = functools.partial(query_grad, devices=devices, cuts=cuts)
    grad_rest = overlap(jobs, work, [back[0] for back in backs], base, g_lat, w_query, rest, grad_out)
    rest_out = Scatter(grid, grad_rest, q_top + k_rows)
    jobs.append(rest_out)
    work = functools.partial(kv_grad, devices=devices)
    grad_kv = overlap(jobs, work, [g for back in backs for g in back[1:]], [side[0] for side in sides])
    kv_out = Scatter(grid, grad_kv, k_rows)
    jobs.append(kv_out)
    inputs_grad = None
    tiles = length // 512
    half = max(tiles // 2, 1)
    for s in range(seqs):
        for at in range(0, tiles, half):
            work = functools.partial(input_grad, s, at, min(half, tiles - at))
            args = (backs[s][1], backs[s][2], kv_weights, g_in, byte_inputs)
            inputs_grad = overlap(jobs, work, *args, *(() if inputs_grad is None else (inputs_grad,)))
    finish(jobs)
    both = jnp.concatenate(mlp_out.parts, axis=0)
    in_grad, back_grad = both[:q_rows], both[q_rows:]
    both = jnp.concatenate(kv_out.parts, axis=0)
    key_grad, value_grad = both[:k_rows], both[k_rows:]
    both = jnp.concatenate(rest_out.parts, axis=0)
    found = {"query": [], "out": [], "latents": []}
    for what, rows_of, columns, at, beside in unpack_rest(both.shape[0], cuts):
        found[what].append((rows_of[0], columns[0], both[at[0] : at[1], beside[0] : beside[1]]))

    def joined(what, axis):
        pieces = sorted(found[what], key=lambda piece: piece[:2])
        return jnp.concatenate([piece[2] for piece in pieces], axis=axis)

    query_grad_mine, out_grad, base_grad = joined("query", 0), joined("out", 1), joined("latents", 1)

    def gain_grad(gain, *pairs):
        total = sum(jnp.sum(g * w.astype(F32), axis=1) for g, w in pairs)
        return total / gain.astype(F32)

    gin_grad = gain_grad(in_gain, (key_grad, key_weight), (value_grad, value_weight))
    glat_grad = gain_grad(lat_gain, (query_grad_mine, query_weight))
    gmlp_grad = gain_grad(mlp_gain, (in_grad, mlp_in_weight))
    return (
        latents,
        inputs_grad,
        base_grad,
        glat_grad,
        query_grad_mine,
        gin_grad,
        key_grad,
        value_grad,
        out_grad,
        gmlp_grad,
        in_grad,
        back_grad,
    )


def solution(mesh):
    in_specs = (
        P("dp", None, None),
        P("dp"),
        P("dp", None),
        P("dp", None, None),
        P("dp", None),
        P("dp"),
        P("dp", None),
        P("dp"),
        P("dp", None),
        P("dp", None),
        P("dp", None),
        P("dp"),
        P("dp", None),
        P("dp", None),
    )
    out_specs = (
        P("dp", None, None),
        P("dp", None, None),
        P("dp", None),
        P("dp"),
        P("dp", None),
        P("dp"),
        P("dp", None),
        P("dp", None),
        P("dp", None),
        P("dp"),
        P("dp", None),
        P("dp", None),
    )
    return jax.shard_map(local, mesh=mesh, in_specs=in_specs, out_specs=out_specs, check_vma=False)
```

time: 396 us -> 324 us (0.82)
  Pallas kernels: 105 us -> 161 us
  local copies, waits for them, and re-layouts: 56.7 us -> 18.5 us
  matrix products: 27 us -> 0 us
  other arithmetic: 45 us -> 23.1 us
  waiting for transfers between devices: 74.3 us -> 53.6 us
  starting transfers between devices: 67 us -> 48.9 us
    pallas_call x5 -> x13, Pallas kernels: 81.1 us -> 133 us  [the longest x4 29.5 us: input_grad(): pl.pallas_call(input_grad_kernel, grid=(steps,), in_specs=specs + [pl.Blo...]
    dot_general x11 -> x0, matrix products: 27 us -> none  [the longest x1 3.62 us: local(): jnp.einsum('sih,sif->hf', act, latents_cot, preferred_element_type=F32)]
    ppermute x48 -> x40, waiting for transfers between devices: 73.9 us -> 53.6 us  [the longest x16 38.6 us: exchange(): lax.ppermute(part[0], 'dp', grid.shift(dim, -r))]
    ppermute x48 -> x40, starting transfers between devices: 67 us -> 48.9 us  [the longest x24 27 us: exchange(): lax.ppermute(piece, 'dp', self.grid.shift(dim, r))]
    convert_element_type x22 -> x15, other arithmetic: 21.8 us -> 4.88 us  [receive(): total.astype(self.wire)]
    concatenate x5 -> x4, local copies, waits for them, and re-layouts: 12.6 us -> 0.81 us  [the longest x1 0.71 us: pack_rest(): join([query[..., :q_top, :], out[..., :width], beside, query[..., q_top:,...]
    unnamed x80 -> x33, local copies, waits for them, and re-layouts: 12.9 us -> 4.69 us
    concatenate x5 -> x11, other arithmetic: 2.56 us -> 10.6 us  [the longest x5 7.25 us: receive(): self.parts = [jnp.concatenate(part, axis=0) for part in got]]
  transfers between devices with their start and end apart: 50 -> 41, of which waited for: 22 -> 16; matrix products, arithmetic and copies ran while one was open for 14% -> 6% of each run, Pallas kernels for 21% -> 43%
where the time goes in v2:
time: 324 us; the launch traced here: 320 us
  Pallas kernels  161 us (50%)
  waiting for transfers between devices  53.6 us (17%)
  starting transfers between devices  48.9 us (15%)
  other arithmetic  23.1 us (7%)
  local copies, waits for them, and re-layouts  18.5 us (6%)
  between operations  15 us (5%)
    ppermute x16, waiting for transfers between devices, exchange(): lax.ppermute(part[0], 'dp', grid.shift(dim, -r))  38.6 us
    pallas_call x4, Pallas kernels, input_grad(): pl.pallas_call(input_grad_kernel, grid=(steps,), in_specs=specs + [pl.Blo...  29.5 us
    pallas_call x2, Pallas kernels, attend_back(): pl.pallas_call(functools.partial(attend_back_kernel, chunk, scale, 1.0 /...  27.9 us
    ppermute x24, starting transfers between devices, exchange(): lax.ppermute(piece, 'dp', self.grid.shift(dim, r))  27 us
    pallas_call x1, Pallas kernels, feed_forward(): pl.pallas_call(functools.partial(feed_forward_kernel, seqs), in_specs=[vm...  22.5 us
    pallas_call x2, Pallas kernels, project(): pl.pallas_call(project_kernel, grid=(slots // tile,), in_specs=[pl.BlockS...  21.9 us
    ppermute x16, starting transfers between devices, exchange(): lax.ppermute(part[0], 'dp', grid.shift(dim, -r))  21.8 us
    pallas_call x1, Pallas kernels, kv_grad(): pl.pallas_call(functools.partial(kv_grad_kernel, seqs), grid=(slots // ti...  20.4 us
  transfers between devices with their start and end apart: 41, of which 16 were waited for; matrix products, arithmetic and copies ran while one was open for 6% of the time, Pallas kernels for 43%

profile of v2, /device:TPU:0, one launch (start us, length us, event | category | flops | bytes accessed | tf_op | source)
XLA Modules:
  0.0 320.1 jit_solution(10510640962889210829)
XLA Ops:
  10.5 5.0 %collective-permute-start = (bf16[1,56,768]{2,1,0:T(8,128)(2,1)S(1)}, bf16[1,56,768]{2,1,0:T(8,128)(2,1)S(1)}, u32[]{:S(2)}, u32[]{:S(2)}) collective-permute-start(bf16[1,56,768]{2,1,0:T(8,128)(2,1)S(1)} %maximum_bitcast_fusion), channel_id=1, source_target_pairs={{0,24},{1,25},{2,26},{3,27},{4,28},{5,29},{6,30},{7,31},{8,0},{9,1... | collective-permute-start | bytes 258056 | tf_op jit(solution)/shard_map/ppermute | solution.py:123
  32.3 10.4 %collective-permute-done.6 = bf16[1,96,768]{2,1,0:T(8,128)(2,1)S(1)} collective-permute-done((bf16[1,96,768]{2,1,0:T(8,128)(2,1)S(1)}, bf16[1,96,768]{2,1,0:T(8,128)(2,1)S(1)}, u32[]{:S(2)}, u32[]{:S(2)}) %collective-permute-start.6) | collective-permute-done | bytes 147488 | tf_op jit(solution)/shard_map/ppermute | solution.py:123
  46.0 9.2 %collective-permute-done.8 = bf16[8,24,768]{2,1,0:T(8,128)(2,1)S(1)} collective-permute-done((bf16[8,24,768]{2,1,0:T(8,128)(2,1)S(1)}, bf16[8,24,768]{2,1,0:T(8,128)(2,1)S(1)}, u32[]{:S(2)}, u32[]{:S(2)}) %collective-permute-start.8) | collective-permute-done | bytes 294944 | tf_op jit(solution)/shard_map/ppermute | solution.py:123
  55.2 3.7 %collective-permute-done.9 = bf16[8,32,768]{2,1,0:T(8,128)(2,1)S(1)} collective-permute-done((bf16[8,32,768]{2,1,0:T(8,128)(2,1)S(1)}, bf16[8,32,768]{2,1,0:T(8,128)(2,1)S(1)}, u32[]{:S(2)}, u32[]{:S(2)}) %collective-permute-start.9) | collective-permute-done | bytes 393248 | tf_op jit(solution)/shard_map/ppermute | solution.py:123
  63.9 5.0 %collective-permute-done.11 = bf16[4,48,768]{2,1,0:T(8,128)(2,1)} collective-permute-done((bf16[4,48,768]{2,1,0:T(8,128)(2,1)S(1)}, bf16[4,48,768]{2,1,0:T(8,128)(2,1)}, u32[]{:S(2)}, u32[]{:S(2)}) %collective-permute-start.11) | collective-permute-done | bytes 294944 | tf_op jit(solution)/shard_map/ppermute | solution.py:123
  75.3 4.0 %prepare_kv.1 = (bf16[1536,768]{1,0:T(8,128)(2,1)}, f32[1,768]{1,0:T(1,128)}, f32[1,1280]{1,0:T(1,128)}, f32[1,1280]{1,0:T(1,128)}) custom-call(s32[2,32]{1,0:T(2,128)} %pad_add_fusion.place_ref, bf16[32,56,768]{2,1,0:T(8,128)(2,1)} %pad_maximum_fusion.1.stack_ref), custom_call_target="tpu_custom_call" | custom-call | bytes 12000000 | tf_op jit(solution)/shard_map/prepare_kv/pallas_call | solution.py:199
  79.4 11.1 %project.2 = (bf16[1,2048,768]{2,1,0:T(8,128)(2,1)}, bf16[1,8,112,2048]{3,2,1,0:T(8,128)(2,1)}, bf16[1,8,112,2048]{3,2,1,0:T(8,128)(2,1)}) custom-call(bf16[2,2048,768]{2,1,0:T(8,128)(2,1)} %x_ref.6, f32[1,768]{1,0:T(1,128)} %get-tuple-element.458.gain_ref, bf16[1536,768]{1,0:T(8,128)(2,1)} %get-tuple-element.457.w_ref, ...), custom_call_target="tpu_custom_call" | custom-call | flops 9663676416 | bytes 15728640 | tf_op jit(solution)/shard_map/project/pallas_call | solution.py:314
  90.4 5.1 %collective-permute-done.13 = bf16[8,48,768]{2,1,0:T(8,128)(2,1)S(1)} collective-permute-done((bf16[8,48,768]{2,1,0:T(8,128)(2,1)S(1)}, bf16[8,48,768]{2,1,0:T(8,128)(2,1)S(1)}, u32[]{:S(2)}, u32[]{:S(2)}) %collective-permute-start.13) | collective-permute-done | bytes 589856 | tf_op jit(solution)/shard_map/ppermute | solution.py:123
  96.0 10.8 %project.3 = (bf16[1,2048,768]{2,1,0:T(8,128)(2,1)}, bf16[1,8,112,2048]{3,2,1,0:T(8,128)(2,1)}, bf16[1,8,112,2048]{3,2,1,0:T(8,128)(2,1)}) custom-call(bf16[2,2048,768]{2,1,0:T(8,128)(2,1)} %x_ref.6, f32[1,768]{1,0:T(1,128)} %get-tuple-element.458.gain_ref, bf16[1536,768]{1,0:T(8,128)(2,1)} %get-tuple-element.457.w_ref, ...), custom_call_target="tpu_custom_call" | custom-call | flops 9663676416 | bytes 15728640 | tf_op jit(solution)/shard_map/project/pallas_call | solution.py:314
  106.8 4.3 %pad_maximum_fusion.stack_ref = bf16[32,96,768]{2,1,0:T(8,128)(2,1)} fusion(bf16[16,96,768]{2,1,0:T(8,128)(2,1)} %collective-permute-done.15, bf16[16,96,768]{2,1,0:T(8,128)(2,1)S(1)} %maximum_maximum_fusion), kind=kLoop, calls=%fused_computation.1 | loop fusion | flops 2359296 | bytes 9437184 | tf_op jit(solution)/shard_map/concatenate | solution.py:129
  111.1 6.1 %prepare_q.1 = (bf16[1280,768]{1,0:T(8,128)(2,1)}, bf16[768,1280]{1,0:T(8,128)(2,1)}, bf16[256,1280]{1,0:T(8,128)(2,1)}, bf16[8,256,112]{2,1,0:T(8,128)(2,1)}, bf16[768,256]{1,0:T(8,128)(2,1)}) custom-call(s32[2,32]{1,0:T(2,128)} %pad_add_fusion.place_ref, bf16[32,96,768]{2,1,0:T(8,128)(2,1)} %pad_maximum_fusion.stack_ref, ...), custom_call_target="tpu_custom_call" | custom-call | bytes 12000000 | tf_op jit(solution)/shard_map/prepare_q/pallas_call | solution.py:282
  117.2 10.0 %attend.3 = (f32[1,256,768]{2,1,0:T(8,128)}, f32[1,8,256,128]{3,2,1,0:T(8,128)}) custom-call(bf16[8,256,112]{2,1,0:T(8,128)(2,1)} %get-tuple-element.335.q_ref, bf16[1,8,112,2048]{3,2,1,0:T(8,128)(2,1)} %get-tuple-element.337.k_ref, bf16[1,8,112,2048]{3,2,1,0:T(8,128)(2,1)} %get-tuple-element.338.v_ref), custom_call_target="tpu_custom_call" | custom-call | flops 6442450944 | bytes 7340032 | tf_op jit(solution)/shard_map/attend/pallas_call | solution.py:367
  127.2 10.4 %attend.2 = (f32[1,256,768]{2,1,0:T(8,128)}, f32[1,8,256,128]{3,2,1,0:T(8,128)}) custom-call(bf16[8,256,112]{2,1,0:T(8,128)(2,1)} %get-tuple-element.335.q_ref, bf16[1,8,112,2048]{3,2,1,0:T(8,128)(2,1)} %get-tuple-element.320.k_ref, bf16[1,8,112,2048]{3,2,1,0:T(8,128)(2,1)} %get-tuple-element.321.v_ref), custom_call_target="tpu_custom_call" | custom-call | flops 6442450944 | bytes 7340032 | tf_op jit(solution)/shard_map/attend/pallas_call | solution.py:367
  137.7 22.5 %feed_forward.1 = (bf16[2,256,1280]{2,1,0:T(8,128)(2,1)}, bf16[32,80,1280]{2,1,0:T(8,128)(2,1)}, bf16[768,1280]{1,0:T(8,128)(2,1)}, f32[256,1280]{1,0:T(8,128)},...) custom-call(f32[1,256,768]{2,1,0:T(8,128)} %get-tuple-element.303.refs_0_, ...), custom_call_target="tpu_custom_call" | custom-call | flops 13086228480 | bytes 24000000 | tf_op jit(solution)/shard_map/feed_forward/pallas_call | solution.py:633
  166.2 13.8 %attend_back.2 = (bf16[1,256,768]{2,1,0:T(8,128)(2,1)}, bf16[1,768,2048]{2,1,0:T(8,128)(2,1)}, bf16[1,768,2048]{2,1,0:T(8,128)(2,1)}) custom-call(bf16[8,256,112]{2,1,0:T(8,128)(2,1)} %get-tuple-element.335.q_ref, bf16[768,256]{1,0:T(8,128)(2,1)} %get-tuple-element.336.qt_ref, bf16[1,8,112,2048]{3,2,1,0:T(8,128)(2,1)} %get-tuple-element.320.k_ref, ...), custom_call_target="tpu_custom_call" | custom-call | flops 16106127360 | bytes 14680064 | tf_op jit(solution)/shard_map/attend_back/pallas_call | solution.py:418
  185.5 14.0 %attend_back.3 = (bf16[1,256,768]{2,1,0:T(8,128)(2,1)}, bf16[1,768,2048]{2,1,0:T(8,128)(2,1)}, bf16[1,768,2048]{2,1,0:T(8,128)(2,1)}) custom-call(bf16[8,256,112]{2,1,0:T(8,128)(2,1)} %get-tuple-element.335.q_ref, bf16[768,256]{1,0:T(8,128)(2,1)} %get-tuple-element.336.qt_ref, bf16[1,8,112,2048]{3,2,1,0:T(8,128)(2,1)} %get-tuple-element.337.k_ref, ...), custom_call_target="tpu_custom_call" | custom-call | flops 16106127360 | bytes 14680064 | tf_op jit(solution)/shard_map/attend_back/pallas_call | solution.py:418
  199.5 4.2 %collective-permute-done.17 = bf16[4,2,40,1280]{3,2,1,0:T(8,128)(2,1)S(1)} collective-permute-done((bf16[4,2,40,1280]{3,2,1,0:T(8,128)(2,1)S(1)}, bf16[4,2,40,1280]{3,2,1,0:T(8,128)(2,1)S(1)}, u32[]{:S(2)}, u32[]{:S(2)}) %collective-permute-start.17) | collective-permute-done | bytes 819232 | tf_op jit(solution)/shard_map/ppermute | solution.py:151
  207.4 8.2 %query_grad.1 = bf16[32,96,768]{2,1,0:T(8,128)(2,1)} custom-call(bf16[1,256,768]{2,1,0:T(8,128)(2,1)} %get-tuple-element.358.refs_0_, bf16[1,256,768]{2,1,0:T(8,128)(2,1)} %get-tuple-element.359.refs_1_, bf16[256,1280]{1,0:T(8,128)(2,1)} %get-tuple-element.360.refs_2_, f32[1,1280]{1,0:T(1,128)} %get-tuple-element.361.glat_ref.refs_3_, ...), custom_call_target="tpu_custom_call" | custom-call | flops 2013265920 | bytes 12000000 | tf_op jit(solution)/shard_map/query_grad/pallas_call | solution.py:513
  226.5 20.4 %kv_grad.1 = bf16[32,48,768]{2,1,0:T(8,128)(2,1)} custom-call(bf16[1,768,2048]{2,1,0:T(8,128)(2,1)} %get-tuple-element.417.refs_0_.dk_ref, bf16[1,768,2048]{2,1,0:T(8,128)(2,1)} %get-tuple-element.418.refs_1_.dv_ref, bf16[1,768,2048]{2,1,0:T(8,128)(2,1)} %get-tuple-element.455.refs_2_.dk_ref, bf16[1,768,2048]{2,1,0:T(8,128)(2,1)} %get-tuple-element.456.refs_3_.dv_ref, ...), custom_call_target="tpu_custom_call" | custom-call | flops 19327352832 | bytes 18874368 | tf_op jit(solution)/shard_map/kv_grad/pallas_call | solution.py:475
  253.8 7.3 %input_grad.4.refs_0_ = bf16[2,2048,768]{2,1,0:T(8,128)(2,1)} custom-call(bf16[1,768,2048]{2,1,0:T(8,128)(2,1)} %get-tuple-element.417.refs_0_.dk_ref, bf16[1,768,2048]{2,1,0:T(8,128)(2,1)} %get-tuple-element.418.refs_1_.dv_ref, bf16[1536,768]{1,0:T(8,128)(2,1)} %get-tuple-element.457.w_ref, f32[1,768]{1,0:T(1,128)} %get-tuple-element.458.gain_ref, ...), custom_call_target="tpu_custom_call" | custom-call | flops 4831838208 | bytes 6291456 | tf_op jit(solution)/shard_map/input_grad/pallas_call | solution.py:542
  261.0 4.8 %collective-permute-done.25 = bf16[4,2,48,768]{3,2,1,0:T(8,128)(2,1)S(1)} collective-permute-done((bf16[4,2,48,768]{3,2,1,0:T(8,128)(2,1)S(1)}, bf16[4,2,48,768]{3,2,1,0:T(8,128)(2,1)S(1)}, u32[]{:S(2)}, u32[]{:S(2)}) %collective-permute-start.25) | collective-permute-done | bytes 589856 | tf_op jit(solution)/shard_map/ppermute | solution.py:151
  272.0 7.7 %input_grad.5.refs_0_ = bf16[2,2048,768]{2,1,0:T(8,128)(2,1)} custom-call(bf16[1,768,2048]{2,1,0:T(8,128)(2,1)} %get-tuple-element.417.refs_0_.dk_ref, bf16[1,768,2048]{2,1,0:T(8,128)(2,1)} %get-tuple-element.418.refs_1_.dv_ref, bf16[1536,768]{1,0:T(8,128)(2,1)} %get-tuple-element.457.w_ref, ...), custom_call_target="tpu_custom_call", output_to_operand_aliasing={{}: (5, {})} | custom-call | flops 4831838208 | bytes 6291456 | tf_op jit(solution)/shard_map/input_grad/pallas_call | solution.py:542
  289.3 7.3 %input_grad.6.refs_0_ = bf16[2,2048,768]{2,1,0:T(8,128)(2,1)} custom-call(bf16[1,768,2048]{2,1,0:T(8,128)(2,1)} %get-tuple-element.455.refs_2_.dk_ref, bf16[1,768,2048]{2,1,0:T(8,128)(2,1)} %get-tuple-element.456.refs_3_.dv_ref, bf16[1536,768]{1,0:T(8,128)(2,1)} %get-tuple-element.457.w_ref, ...), custom_call_target="tpu_custom_call", output_to_operand_aliasing={{}: (5, {})} | custom-call | flops 4831838208 | bytes 6291456 | tf_op jit(solution)/shard_map/input_grad/pallas_call | solution.py:542
  303.9 7.3 %input_grad.7 = bf16[2,2048,768]{2,1,0:T(8,128)(2,1)} custom-call(bf16[1,768,2048]{2,1,0:T(8,128)(2,1)} %get-tuple-element.455.refs_2_.dk_ref, bf16[1,768,2048]{2,1,0:T(8,128)(2,1)} %get-tuple-element.456.refs_3_.dv_ref, bf16[1536,768]{1,0:T(8,128)(2,1)} %get-tuple-element.457.w_ref, ...), custom_call_target="tpu_custom_call", output_to_operand_aliasing={{}: (5, {})} | custom-call | flops 4831838208 | bytes 6291456 | tf_op jit(solution)/shard_map/input_grad/pallas_call | solution.py:542
  (207 shorter events, 92.5 us)
Async XLA Ops:
  7.2 130.5 %all-gather.2.cloned.1.call-start = ((), (), s32[]{:S(2)}) async-start(), calls=%async_computation | async-start | bytes 6758400 | tf_op jit(solution)/shard_map/all_gather | solution.py:671
  25.6 17.1 %collective-permute-start.6 = (bf16[1,96,768]{2,1,0:T(8,128)(2,1)S(1)}, bf16[1,96,768]{2,1,0:T(8,128)(2,1)S(1)}, u32[]{:S(2)}, u32[]{:S(2)}) collective-permute-start(bf16[1,96,768]{2,1,0:T(8,128)(2,1)S(1)} %bitcast.117), channel_id=1, source_target_pairs={{0,16},{1,17},{2,18},{3,19},{4,20},{5,21},{6,22},{7,23},{8,24},{9,... | collective-permute-start | bytes 442376 | tf_op jit(solution)/shard_map/ppermute | solution.py:123
  25.7 17.0 %collective-permute-start.7 = (bf16[1,96,768]{2,1,0:T(8,128)(2,1)S(1)}, bf16[1,96,768]{2,1,0:T(8,128)(2,1)S(1)}, u32[]{:S(2)}, u32[]{:S(2)}) collective-permute-start(bf16[1,96,768]{2,1,0:T(8,128)(2,1)S(1)} %bitcast.118), channel_id=1, source_target_pairs={{0,8},{1,9},{2,10},{3,11},{4,12},{5,13},{6,14},{7,15},{8,16},{9,17... | collective-permute-start | bytes 442376 | tf_op jit(solution)/shard_map/ppermute | solution.py:123
  27.7 15.1 %collective-permute-start.4 = (bf16[4,32,768]{2,1,0:T(8,128)(2,1)S(1)}, bf16[4,32,768]{2,1,0:T(8,128)(2,1)S(1)}, u32[]{:S(2)}, u32[]{:S(2)}) collective-permute-start(bf16[4,32,768]{2,1,0:T(8,128)(2,1)S(1)} %split.41), channel_id=1, source_target_pairs={{0,4},{1,5},{2,6},{3,7},{4,0},{5,1},{6,2},{7,3},{8,12},{9,13},{10,... | collective-permute-start | bytes 589832 | tf_op jit(solution)/shard_map/ppermute | solution.py:123
  29.2 13.5 %collective-permute-start.3 = (bf16[4,24,768]{2,1,0:T(8,128)(2,1)S(1)}, bf16[4,24,768]{2,1,0:T(8,128)(2,1)S(1)}, u32[]{:S(2)}, u32[]{:S(2)}) collective-permute-start(bf16[4,24,768]{2,1,0:T(8,128)(2,1)S(1)} %split.40), channel_id=1, source_target_pairs={{0,2},{1,3},{2,0},{3,1},{4,6},{5,7},{6,4},{7,5},{8,10},{9,11},{10,... | collective-permute-start | bytes 442376 | tf_op jit(solution)/shard_map/ppermute | solution.py:123
  42.8 16.1 %collective-permute-start.9 = (bf16[8,32,768]{2,1,0:T(8,128)(2,1)S(1)}, bf16[8,32,768]{2,1,0:T(8,128)(2,1)S(1)}, u32[]{:S(2)}, u32[]{:S(2)}) collective-permute-start(bf16[8,32,768]{2,1,0:T(8,128)(2,1)S(1)} %pad_maximum_fusion.4), channel_id=1, source_target_pairs={{0,2},{1,3},{2,0},{3,1},{4,6},{5,7},{6,4},{7,5},{8,10},{9,11},{10,... | collective-permute-start | bytes 1179656 | tf_op jit(solution)/shard_map/ppermute | solution.py:123
  73.1 22.4 %collective-permute-start.13 = (bf16[8,48,768]{2,1,0:T(8,128)(2,1)S(1)}, bf16[8,48,768]{2,1,0:T(8,128)(2,1)S(1)}, u32[]{:S(2)}, u32[]{:S(2)}) collective-permute-start(bf16[8,48,768]{2,1,0:T(8,128)(2,1)S(1)} %get-tuple-element.283), channel_id=1, source_target_pairs={{0,4},{1,5},{2,6},{3,7},{4,0},{5,1},{6,2},{7,3},{8,12},{9,13},{10,... | collective-permute-start | bytes 1769480 | tf_op jit(solution)/shard_map/ppermute | solution.py:123
  74.6 21.0 %collective-permute-start.14 = (bf16[8,48,768]{2,1,0:T(8,128)(2,1)S(1)}, bf16[8,48,768]{2,1,0:T(8,128)(2,1)S(1)}, u32[]{:S(2)}, u32[]{:S(2)}) collective-permute-start(bf16[8,48,768]{2,1,0:T(8,128)(2,1)S(1)} %get-tuple-element.285), channel_id=1, source_target_pairs={{0,2},{1,3},{2,0},{3,1},{4,6},{5,7},{6,4},{7,5},{8,10},{9,11},{10,... | collective-permute-start | bytes 1769480 | tf_op jit(solution)/shard_map/ppermute | solution.py:123
  165.7 14.3 %collective-permute-start.16 = (bf16[4,2,2,80,1280]{4,3,2,0,1:T(8,128)(2,1)}, bf16[4,2,2,80,1280]{4,3,2,0,1:T(8,128)(2,1)}, u32[]{:S(2)}, u32[]{:S(2)}) collective-permute-start(bf16[4,2,2,80,1280]{4,3,2,0,1:T(8,128)(2,1)} %bitcast.90), channel_id=1, source_target_pairs={{0,1},{1,0},{2,3},{3,2},{4,5},{5,4},{6,7},{7,6},{8,9},{9,8},{10,11... | collective-permute-start | bytes 9830408 | tf_op jit(solution)/shard_map/ppermute | solution.py:151
  183.4 20.3 %collective-permute-start.17 = (bf16[4,2,40,1280]{3,2,1,0:T(8,128)(2,1)S(1)}, bf16[4,2,40,1280]{3,2,1,0:T(8,128)(2,1)S(1)}, u32[]{:S(2)}, u32[]{:S(2)}) collective-permute-start(bf16[4,2,40,1280]{3,2,1,0:T(8,128)(2,1)S(1)} %get-tuple-element.332), channel_id=1, source_target_pairs={{0,4},{1,5},{2,6},{3,7},{4,0},{5,1},{6,2},{7,3},{8,12},{9,13},{10,... | collective-permute-start | bytes 2457608 | tf_op jit(solution)/shard_map/ppermute | solution.py:151
  184.9 20.0 %collective-permute-start.18 = (bf16[4,2,40,1280]{3,2,1,0:T(8,128)(2,1)S(1)}, bf16[4,2,40,1280]{3,2,1,0:T(8,128)(2,1)S(1)}, u32[]{:S(2)}, u32[]{:S(2)}) collective-permute-start(bf16[4,2,40,1280]{3,2,1,0:T(8,128)(2,1)S(1)} %bitcast.113), channel_id=1, source_target_pairs={{0,2},{1,3},{2,0},{3,1},{4,6},{5,7},{6,4},{7,5},{8,10},{9,11},{10,... | collective-permute-start | bytes 2457608 | tf_op jit(solution)/shard_map/ppermute | solution.py:151
  221.1 25.8 %collective-permute-start.24 = (bf16[4,2,2,96,768]{4,3,2,0,1:T(8,128)(2,1)S(1)}, bf16[4,2,2,96,768]{4,3,2,0,1:T(8,128)(2,1)S(1)}, u32[]{:S(2)}, u32[]{:S(2)}) collective-permute-start(bf16[4,2,2,96,768]{4,3,2,0,1:T(8,128)(2,1)S(1)} %bitcast.110), channel_id=1, source_target_pairs={{0,1},{1,0},{2,3},{3,2},{4,5},{5,4},{6,7},{7,6},{8,9},{9,8},{10,11... | collective-permute-start | bytes 7077896 | tf_op jit(solution)/shard_map/ppermute | solution.py:151
  221.1 25.8 %collective-permute-start.21 = (bf16[80,1280]{1,0:T(8,128)(2,1)}, bf16[80,1280]{1,0:T(8,128)(2,1)S(1)}, u32[]{:S(2)}, u32[]{:S(2)}) collective-permute-start(bf16[80,1280]{1,0:T(8,128)(2,1)} %get-tuple-element.377), channel_id=1, source_target_pairs={{0,8},{1,9},{2,10},{3,11},{4,12},{5,13},{6,14},{7,15},{8,16},{9,17... | collective-permute-start | bytes 614408 | tf_op jit(solution)/shard_map/ppermute | solution.py:151
  222.6 24.3 %collective-permute-start.22 = (bf16[80,1280]{1,0:T(8,128)(2,1)}, bf16[80,1280]{1,0:T(8,128)(2,1)S(1)}, u32[]{:S(2)}, u32[]{:S(2)}) collective-permute-start(bf16[80,1280]{1,0:T(8,128)(2,1)} %get-tuple-element.378), channel_id=1, source_target_pairs={{0,16},{1,17},{2,18},{3,19},{4,20},{5,21},{6,22},{7,23},{8,24},{9,... | collective-permute-start | bytes 614408 | tf_op jit(solution)/shard_map/ppermute | solution.py:151
  224.2 22.7 %collective-permute-start.23 = (bf16[80,1280]{1,0:T(8,128)(2,1)S(1)}, bf16[80,1280]{1,0:T(8,128)(2,1)S(1)}, u32[]{:S(2)}, u32[]{:S(2)}) collective-permute-start(bf16[80,1280]{1,0:T(8,128)(2,1)S(1)} %get-tuple-element.379), channel_id=1, source_target_pairs={{0,24},{1,25},{2,26},{3,27},{4,28},{5,29},{6,30},{7,31},{8,0},{9,1... | collective-permute-start | bytes 614408 | tf_op jit(solution)/shard_map/ppermute | solution.py:151
  250.0 16.9 %collective-permute-start.27 = (bf16[4,2,2,48,768]{4,3,2,0,1:T(8,128)(2,1)S(1)}, bf16[4,2,2,48,768]{4,3,2,0,1:T(8,128)(2,1)S(1)}, u32[]{:S(2)}, u32[]{:S(2)}) collective-permute-start(bf16[4,2,2,48,768]{4,3,2,0,1:T(8,128)(2,1)S(1)} %bitcast.112), channel_id=1, source_target_pairs={{0,1},{1,0},{2,3},{3,2},{4,5},{5,4},{6,7},{7,6},{8,9},{9,8},{10,11... | collective-permute-start | bytes 3538952 | tf_op jit(solution)/shard_map/ppermute | solution.py:151
  250.1 15.7 %collective-permute-start.25 = (bf16[4,2,48,768]{3,2,1,0:T(8,128)(2,1)S(1)}, bf16[4,2,48,768]{3,2,1,0:T(8,128)(2,1)S(1)}, u32[]{:S(2)}, u32[]{:S(2)}) collective-permute-start(bf16[4,2,48,768]{3,2,1,0:T(8,128)(2,1)S(1)} %get-tuple-element.392), channel_id=1, source_target_pairs={{0,4},{1,5},{2,6},{3,7},{4,0},{5,1},{6,2},{7,3},{8,12},{9,13},{10,... | collective-permute-start | bytes 1769480 | tf_op jit(solution)/shard_map/ppermute | solution.py:151
  251.5 15.4 %collective-permute-start.26 = (bf16[4,2,48,768]{3,2,1,0:T(8,128)(2,1)S(1)}, bf16[4,2,48,768]{3,2,1,0:T(8,128)(2,1)S(1)}, u32[]{:S(2)}, u32[]{:S(2)}) collective-permute-start(bf16[4,2,48,768]{3,2,1,0:T(8,128)(2,1)S(1)} %bitcast.114), channel_id=1, source_target_pairs={{0,2},{1,3},{2,0},{3,1},{4,6},{5,7},{6,4},{7,5},{8,10},{9,11},{10,... | collective-permute-start | bytes 1769480 | tf_op jit(solution)/shard_map/ppermute | solution.py:151
  270.1 12.9 %collective-permute-start.30 = (bf16[4,2,24,768]{3,2,1,0:T(8,128)(2,1)S(1)}, bf16[4,2,24,768]{3,2,1,0:T(8,128)(2,1)S(1)}, u32[]{:S(2)}, u32[]{:S(2)}) collective-permute-start(bf16[4,2,24,768]{3,2,1,0:T(8,128)(2,1)S(1)} %get-tuple-element.414), channel_id=1, source_target_pairs={{0,4},{1,5},{2,6},{3,7},{4,0},{5,1},{6,2},{7,3},{8,12},{9,13},{10,... | collective-permute-start | bytes 884744 | tf_op jit(solution)/shard_map/ppermute | solution.py:151
  270.7 12.3 %collective-permute-start.31 = (bf16[4,2,24,768]{3,2,1,0:T(8,128)(2,1)S(1)}, bf16[4,2,24,768]{3,2,1,0:T(8,128)(2,1)S(1)}, u32[]{:S(2)}, u32[]{:S(2)}) collective-permute-start(bf16[4,2,24,768]{3,2,1,0:T(8,128)(2,1)S(1)} %bitcast.115), channel_id=1, source_target_pairs={{0,2},{1,3},{2,0},{3,1},{4,6},{5,7},{6,4},{7,5},{8,10},{9,11},{10,... | collective-permute-start | bytes 884744 | tf_op jit(solution)/shard_map/ppermute | solution.py:151
  283.4 13.1 %collective-permute-start.32 = (bf16[96,768]{1,0:T(8,128)(2,1)S(1)}, bf16[96,768]{1,0:T(8,128)(2,1)S(1)}, u32[]{:S(2)}, u32[]{:S(2)}) collective-permute-start(bf16[96,768]{1,0:T(8,128)(2,1)S(1)} %get-tuple-element.433), channel_id=1, source_target_pairs={{0,8},{1,9},{2,10},{3,11},{4,12},{5,13},{6,14},{7,15},{8,16},{9,17... | collective-permute-start | bytes 442376 | tf_op jit(solution)/shard_map/ppermute | solution.py:151
  283.9 12.6 %collective-permute-start.33 = (bf16[96,768]{1,0:T(8,128)(2,1)S(1)}, bf16[96,768]{1,0:T(8,128)(2,1)S(1)}, u32[]{:S(2)}, u32[]{:S(2)}) collective-permute-start(bf16[96,768]{1,0:T(8,128)(2,1)S(1)} %get-tuple-element.434), channel_id=1, source_target_pairs={{0,16},{1,17},{2,18},{3,19},{4,20},{5,21},{6,22},{7,23},{8,24},{9,... | collective-permute-start | bytes 442376 | tf_op jit(solution)/shard_map/ppermute | solution.py:151
  296.9 14.9 %collective-permute-start.37 = (bf16[48,768]{1,0:T(8,128)(2,1)S(1)}, bf16[48,768]{1,0:T(8,128)(2,1)S(1)}, u32[]{:S(2)}, u32[]{:S(2)}) collective-permute-start(bf16[48,768]{1,0:T(8,128)(2,1)S(1)} %get-tuple-element.452), channel_id=1, source_target_pairs={{0,8},{1,9},{2,10},{3,11},{4,12},{5,13},{6,14},{7,15},{8,16},{9,17... | collective-permute-start | bytes 221192 | tf_op jit(solution)/shard_map/ppermute | solution.py:151
  298.8 12.9 %collective-permute-start.38 = (bf16[48,768]{1,0:T(8,128)(2,1)S(1)}, bf16[48,768]{1,0:T(8,128)(2,1)S(1)}, u32[]{:S(2)}, u32[]{:S(2)}) collective-permute-start(bf16[48,768]{1,0:T(8,128)(2,1)S(1)} %get-tuple-element.453), channel_id=1, source_target_pairs={{0,16},{1,17},{2,18},{3,19},{4,20},{5,21},{6,22},{7,23},{8,24},{9,... | collective-permute-start | bytes 221192 | tf_op jit(solution)/shard_map/ppermute | solution.py:151
  (29 other events, 247.1 us)
Sparse Core Ops, SparseCore 0:
  11.4 90.9 all-gather.1
